TPU v7x, 128 devices: a whole 4x4x4 slice. The times are simulated.
128 devices in a mesh: section: 2 (over x_lo), expert: 16 (over z, x_hi, core), dp: 4 (over y).
Axes of the slice: x: 4 (x_hi: 2, x_lo: 2; x = x_hi * 2 + x_lo), y: 4, z: 4, core: 2. Of those that a mesh axis runs over, the one named last changes fastest.
Arguments:
- fresh_tokens: bfloat16 [2, 4096, 4096], P(None, ('expert', 'dp')), may hold values from -60 to 60
- in_flight: bfloat16 [4096, 4096], P(('expert', 'dp')), may hold values from -60 to 60
- norm_weight: float32 [2, 4096], P('section'), may hold values from 0.1 to 1.9
- gate_up: bfloat16 [2, 16, 2, 4096, 768], P('section', 'expert', None, 'dp'), may hold values from -0.09375 to 0.09375
- down_proj: bfloat16 [2, 16, 768, 4096], P('section', 'expert', 'dp'), may hold values from -0.21875 to 0.21875
- first_moment: bfloat16 [2, 16, 768, 4096], P('section', 'expert', 'dp'), may hold values from -6 to 6
- second_moment: bfloat16 [2, 16, 768, 4096], P('section', 'expert', 'dp'), may hold values from 0.099609375 to 4
- route_ids: int32 [2, 2, 4096, 8], P('section', None, ('expert', 'dp')), may hold values from 0 to 15, all different within a row; in each aligned block of 64 rows (0 to 63, 64 to 127, ..., all dimensions but the last counted through in order) at most 36 rows name the same one
- route_probs: float32 [2, 2, 4096, 8], P('section', None, ('expert', 'dp')), may hold values from 0.05 to 1
- trade_flags: int32 [8, 1], replicated, may hold values from 0 to 1, as said below
Outputs:
- layer_out: bfloat16 [2, 2, 4096, 4096], P('section', None, ('expert', 'dp'))
- gate_up_moved: bfloat16 [2, 16, 2, 4096, 768], P('section', 'expert', None, 'dp')
- down_moved: bfloat16 [2, 16, 768, 4096], P('section', 'expert', 'dp')
- first_moved: bfloat16 [2, 16, 768, 4096], P('section', 'expert', 'dp')
- second_moved: bfloat16 [2, 16, 768, 4096], P('section', 'expert', 'dp')
Inputs may be any that keep to these rules, and one draw needn't show every extreme that they name: `route_ids`: in each aligned block of 64 rows (one device's tokens of one section and tick) the 8 experts of a token differ and no expert is chosen by more than 36 rows. `trade_flags`: at least one entry is 1 and at least one is 0.
All inputs are finite; a program needn't handle non-finite values.
Results may differ from a plain program's by a relative error of at most 0.0035.
Values may be sent and summed in bfloat16 or wider, within the bound.
A program may use at most 128 MiB of HBM per device.

v0:
```python
import jax
import jax.numpy as jnp
from jax import lax
from jax.sharding import PartitionSpec as P

EXPERTS = 16
TOPK = 8
CAP = 36


def partner(value, axis, bit):
    return lax.ppermute(value, axis, [(i, i ^ 1 << bit) for i in range(lax.axis_size(axis))])


def shifted(block, axis, distance):
    devices = range(lax.axis_size(axis))
    route = [(i - distance, i) for i in devices if i - distance in devices]
    return lax.ppermute(block, axis, route)


def rms_normed(inputs, norm_gain):
    values = inputs.astype(jnp.float32)
    inverse_rms = lax.rsqrt(jnp.mean(values * values, axis=-1, keepdims=True) + 1e-06)
    return (values * inverse_rms * norm_gain).astype(jnp.bfloat16)


def per_device(
    fresh_tokens,
    in_flight,
    norm_weight,
    gate_up,
    down_proj,
    first_moment,
    second_moment,
    route_ids,
    route_probs,
    trade_flags,
):
    groups = lax.axis_size("expert")
    half_span = groups // 2
    top_bit = groups.bit_length() - 2
    own_rank = lax.axis_index("expert")
    section_index = lax.axis_index("section")
    experts_here = gate_up.shape[1]
    width = fresh_tokens.shape[2]
    own_flags = trade_flags[own_rank % half_span] == 1
    mask_five = own_flags[None, :, None, None, None]
    mask_four = own_flags[None, :, None, None]
    traded = partner((gate_up, down_proj, first_moment, second_moment), "expert", top_bit)
    gate_up_moved = jnp.where(mask_five, traded[0], gate_up)
    down_moved = jnp.where(mask_four, traded[1], down_proj)
    first_moved = jnp.where(mask_four, traded[2], first_moment)
    second_moved = jnp.where(mask_four, traded[3], second_moment)
    expert_ids = jnp.arange(EXPERTS, dtype=jnp.int32)
    home_block = expert_ids // experts_here
    home_slot = expert_ids % experts_here
    local_gate_up, local_down = (gate_up_moved, down_moved)
    expert_flags = trade_flags[home_block % half_span, home_slot]
    holder = jnp.where(expert_flags == 1, home_block ^ half_span, home_block)
    full_gate_up, full_down = (
        lax.all_gather(local_gate_up, "dp", axis=3, tiled=True),
        lax.all_gather(local_down, "dp", axis=2, tiled=True),
    )
    gate_weights = full_gate_up[0, :, 0]
    up_weights = full_gate_up[0, :, 1]
    down_weights = full_down[0]

    def expert_work(arrived):
        gate_part = jnp.einsum(
            "sicd,idf->sicf", arrived, gate_weights, preferred_element_type=jnp.float32
        )
        up_part = jnp.einsum(
            "sicd,idf->sicf", arrived, up_weights, preferred_element_type=jnp.float32
        )
        active = (jax.nn.silu(gate_part) * up_part).astype(jnp.bfloat16)
        result = jnp.einsum(
            "sicf,ifd->sicd", active, down_weights, preferred_element_type=jnp.float32
        ).astype(jnp.bfloat16)
        return lax.all_to_all(result, "expert", split_axis=0, concat_axis=0, tiled=True)

    def layer(inputs, layer_ids, layer_probs):
        normed = rms_normed(inputs, norm_weight[0])
        mix_weight = layer_probs / jnp.sum(layer_probs, axis=-1, keepdims=True)
        flat_ids = layer_ids.reshape(-1)
        one_hot = (flat_ids[:, None] == expert_ids[None, :]).astype(jnp.int32)
        slot_index = jnp.sum((jnp.cumsum(one_hot, axis=0) - 1) * one_hot, axis=1)
        target = holder[flat_ids]
        position = (target * experts_here + flat_ids % experts_here) * CAP + slot_index
        token_rows = jnp.arange(flat_ids.shape[0], dtype=jnp.int32) // TOPK
        outgoing = jnp.zeros((groups * experts_here * CAP, width), jnp.bfloat16)
        outgoing = outgoing.at[position].set(normed[token_rows])
        outgoing = outgoing.reshape(groups, experts_here, CAP, width)
        returned = expert_work(
            lax.all_to_all(outgoing, "expert", split_axis=0, concat_axis=0, tiled=True)
        )
        rows_back = returned.reshape(-1, width)[position].astype(jnp.float32)
        combined = jnp.sum(mix_weight[:, :, None] * rows_back.reshape(-1, TOPK, width), axis=1)
        return (inputs.astype(jnp.float32) + combined).astype(jnp.bfloat16)

    first_input = jnp.where(section_index == 0, fresh_tokens[0], in_flight)
    tick_zero = layer(first_input, route_ids[0, 0], route_probs[0, 0])
    arrived = shifted(tick_zero, "section", 1)
    second_input = jnp.where(section_index == 0, fresh_tokens[1], arrived)
    tick_one = layer(second_input, route_ids[0, 1], route_probs[0, 1])
    layer_out = jnp.stack([tick_zero, tick_one])[None]
    return (layer_out, gate_up_moved, down_moved, first_moved, second_moved)


def solution(mesh):
    return jax.shard_map(
        per_device,
        mesh=mesh,
        in_specs=(
            P(None, ("expert", "dp"), None),
            P(("expert", "dp"), None),
            P("section", None),
            P("section", "expert", None, "dp", None),
            P("section", "expert", "dp", None),
            P("section", "expert", "dp", None),
            P("section", "expert", "dp", None),
            P("section", None, ("expert", "dp"), None),
            P("section", None, ("expert", "dp"), None),
            P(),
        ),
        out_specs=(
            P("section", None, ("expert", "dp"), None),
            P("section", "expert", None, "dp", None),
            P("section", "expert", "dp", None),
            P("section", "expert", "dp", None),
            P("section", "expert", "dp", None),
        ),
        check_vma=False,
    )
```

profile of v0, /device:TPU:2, one launch (start us, length us, event | category | flops | bytes accessed | tf_op | source)
XLA Modules:
  0.0 677.9 jit_solution(17666635788543206956)
XLA Ops:
  12.5 67.0 %collective-permute-done.1 = bf16[1,1,2,1024,768]{4,3,2,1,0:T(8,128)(2,1)S(1)} collective-permute-done((bf16[1,1,2,1024,768]{4,3,2,1,0:T(8,128)(2,1)}, bf16[1,1,2,1024,768]{4,3,2,1,0:T(8,128)(2,1)S(1)}, u32[]{:S(2)}, u32[]{:S(2)}) %collective-permute-start.1) | collective-permute-done | bytes 3145760 | tf_op jit(solution)/shard_map/ppermute | solution.py:12
  93.5 5.8 fusion.58
  100.7 20.5 %collective-permute-done = bf16[1,1,192,4096]{3,2,1,0:T(8,128)(2,1)} collective-permute-done((bf16[1,1,192,4096]{3,2,1,0:T(8,128)(2,1)}, bf16[1,1,192,4096]{3,2,1,0:T(8,128)(2,1)}, u32[]{:S(2)}, u32[]{:S(2)}) %collective-permute-start) | collective-permute-done | bytes 1572896 | tf_op jit(solution)/shard_map/ppermute | solution.py:12
  124.9 21.3 %scatter_custom_fusion = bf16[576,4096]{1,0:T(8,128)(2,1)} fusion(s32[512]{0:T(512)S(1)} %bitcast.214, bf16[64,4096]{1,0:T(8,128)(2,1)S(1)} %fusion.44, s32[1024]{0:T(1024)S(1)} %pad_clamp_fusion.2, bf16[]{:T(256)} %constant.121.clone.1), kind=kCustom, calls=%fused_computation.29 | custom fusion | bytes 4718594 | tf_op jit(solution)/shard_map/scatter | solution.py:91
  146.2 7.3 %reshape.360 = bf16[16,1,36,4096]{3,2,0,1:T(8,128)(2,1)} reshape(bf16[576,4096]{1,0:T(8,128)(2,1)} %scatter_custom_fusion) | data formatting | bytes 9437184 | tf_op jit(solution)/shard_map/reshape | solution.py:92
  153.5 68.1 %all_to_all.20 = bf16[16,1,36,4096]{3,2,1,0:T(8,128)(2,1)} all-to-all(bf16[16,1,36,4096]{3,2,1,0:T(8,128)(2,1)} %bitcast.209), channel_id=1, replica_groups=mesh['section'=2,'expert'=16,'dp'=4] {'expert'}, dimensions={0} | all-to-all | bytes 9437184 | tf_op jit(solution)/shard_map/all_to_all | solution.py:94
  221.6 8.2 %fusion.11 = f32[768,16,36]{0,2,1:T(8,128)S(1)} fusion(bf16[1,1,2,4096,768]{4,3,2,1,0:T(8,128)(2,1)} %all-gather.5.cloned.1.call-done, bf16[16,1,36,4096]{3,2,1,0:T(8,128)(2,1)} %all_to_all.20), kind=kOutput, calls=%fused_computation.20 | convolution fusion | flops 3623878656 | bytes 13303808 | tf_op jit(solution)/shard_map/sicd,idf->sicf/dot_general | solution.py:69
  235.9 37.7 %all-gather.3.cloned.1.call-done = bf16[1,1,768,4096]{3,2,1,0:T(8,128)(2,1)} async-done(((bf16[1,1,192,4096]{3,2,1,0:T(8,128)(2,1)}), bf16[1,1,768,4096]{3,2,1,0:T(8,128)(2,1)}) %all-gather.3.cloned.1.call-update) | async-done | bytes 6291472 | tf_op jit(solution)/shard_map/all_gather | solution.py:62
  273.5 8.7 %fusion.4 = bf16[16,1,36,4096]{3,2,1,0:T(8,128)(2,1)} fusion(bf16[16,36,768]{2,1,0:T(8,128)(2,1)S(1)} %fusion.36, bf16[1,1,768,4096]{3,2,1,0:T(8,128)(2,1)} %all-gather.3.cloned.1.call-done), kind=kOutput, calls=%fused_computation.17 | convolution fusion | flops 3626237952 | bytes 11894784 | tf_op jit(solution)/shard_map/sicf,ifd->sicd/dot_general | solution.py:76
  282.3 6.6 all-to-all-start.1
  290.7 61.3 %all-to-all-done.1 = bf16[16,1,36,4096]{3,2,1,0:T(8,128)(2,1)} async-done(((bf16[16,1,36,4096]{3,2,1,0:T(8,128)(2,1)}), bf16[16,1,36,4096]{3,2,1,0:T(8,128)(2,1)}, u32[]{:S(2)}, u32[]{:S(2)}) %all-to-all-start.1) | async-done | bytes 4718624 | tf_op jit(solution)/shard_map/all_to_all | solution.py:79
  352.0 7.3 %reshape.364 = bf16[576,4096]{1,0:T(8,128)(2,1)} reshape(bf16[16,1,36,4096]{3,2,1,0:T(8,128)(2,1)} %all-to-all-done.1) | data formatting | bytes 9437184 | tf_op jit(solution)/shard_map/reshape | solution.py:96
  359.3 11.5 %gather_fusion.1 = bf16[512,4096]{1,0:T(8,128)(2,1)} fusion(bf16[576,4096]{1,0:T(8,128)(2,1)} %reshape.364, s32[1024]{0:T(1024)S(1)} %pad_clamp_fusion.1), kind=kCustom, calls=%fused_computation.2 | custom fusion | bytes 8390656 | tf_op jit(solution)/shard_map/gather | solution.py:96
  378.2 5.8 fusion.57
  383.9 8.0 %collective-permute-done.2 = bf16[64,4096]{1,0:T(8,128)(2,1)S(1)} collective-permute-done((bf16[64,4096]{1,0:T(8,128)(2,1)S(1)}, bf16[64,4096]{1,0:T(8,128)(2,1)S(1)}, u32[]{:S(2)}, u32[]{:S(2)}) %collective-permute-start.2) | collective-permute-done | bytes 524320 | tf_op jit(solution)/shard_map/ppermute | solution.py:18
  392.4 21.4 %scatter_custom_fusion.1 = bf16[576,4096]{1,0:T(8,128)(2,1)} fusion(s32[512]{0:T(512)S(1)} %bitcast.216, bf16[64,4096]{1,0:T(8,128)(2,1)S(1)} %fusion.48, s32[1024]{0:T(1024)S(1)} %pad_clamp_fusion.2, bf16[]{:T(256)} %constant.121.clone.1), kind=kCustom, calls=%fused_computation.27 | custom fusion | bytes 4718594 | tf_op jit(solution)/shard_map/scatter | solution.py:91
  413.8 7.2 %reshape.366 = bf16[16,1,36,4096]{3,2,0,1:T(8,128)(2,1)} reshape(bf16[576,4096]{1,0:T(8,128)(2,1)} %scatter_custom_fusion.1) | data formatting | bytes 9437184 | tf_op jit(solution)/shard_map/reshape | solution.py:92
  421.0 67.3 %all_to_all.21 = bf16[16,1,36,4096]{3,2,1,0:T(8,128)(2,1)S(1)} all-to-all(bf16[16,1,36,4096]{3,2,1,0:T(8,128)(2,1)} %bitcast.210), channel_id=1, replica_groups=mesh['section'=2,'expert'=16,'dp'=4] {'expert'}, dimensions={0} | all-to-all | bytes 9437184 | tf_op jit(solution)/shard_map/all_to_all | solution.py:94
  488.4 6.9 %fusion.10 = f32[768,16,36]{0,2,1:T(8,128)S(1)} fusion(bf16[1,1,2,4096,768]{4,3,2,1,0:T(8,128)(2,1)} %all-gather.5.cloned.1.call-done, bf16[16,1,36,4096]{3,2,1,0:T(8,128)(2,1)S(1)} %all_to_all.21), kind=kOutput, calls=%fused_computation.19 | convolution fusion | flops 3623878656 | bytes 12779520 | tf_op jit(solution)/shard_map/sicd,idf->sicf/dot_general | solution.py:69
  500.0 8.9 %fusion.7 = bf16[16,1,36,4096]{3,2,1,0:T(8,128)(2,1)} fusion(bf16[16,36,768]{2,1,0:T(8,128)(2,1)S(1)} %fusion.39, bf16[1,1,768,4096]{3,2,1,0:T(8,128)(2,1)} %all-gather.3.cloned.1.call-done), kind=kOutput, calls=%fused_computation.18 | convolution fusion | flops 3626237952 | bytes 11894784 | tf_op jit(solution)/shard_map/sicf,ifd->sicd/dot_general | solution.py:76
  517.4 91.1 %collective-permute-done.4 = bf16[1,1,192,4096]{3,2,1,0:T(8,128)(2,1)} collective-permute-done((bf16[1,1,192,4096]{3,2,1,0:T(8,128)(2,1)S(1)}, bf16[1,1,192,4096]{3,2,1,0:T(8,128)(2,1)}, u32[]{:S(2)}, u32[]{:S(2)}) %collective-permute-start.4) | collective-permute-done | bytes 1572896 | tf_op jit(solution)/shard_map/ppermute | solution.py:12
  611.9 29.8 %collective-permute-done.3 = bf16[1,1,192,4096]{3,2,1,0:T(8,128)(2,1)} collective-permute-done((bf16[1,1,192,4096]{3,2,1,0:T(8,128)(2,1)}, bf16[1,1,192,4096]{3,2,1,0:T(8,128)(2,1)}, u32[]{:S(2)}, u32[]{:S(2)}) %collective-permute-start.3) | collective-permute-done | bytes 1572896 | tf_op jit(solution)/shard_map/ppermute | solution.py:12
  645.2 7.2 %reshape.369 = bf16[576,4096]{1,0:T(8,128)(2,1)} reshape(bf16[16,1,36,4096]{3,2,1,0:T(8,128)(2,1)} %all-to-all-done.3) | data formatting | bytes 9437184 | tf_op jit(solution)/shard_map/reshape | solution.py:96
  652.5 11.5 %gather_fusion.2 = bf16[512,4096]{1,0:T(8,128)(2,1)} fusion(bf16[576,4096]{1,0:T(8,128)(2,1)} %reshape.369, s32[1024]{0:T(1024)S(1)} %pad_clamp_fusion), kind=kCustom, calls=%fused_computation.4 | custom fusion | bytes 8390656 | tf_op jit(solution)/shard_map/gather | solution.py:96
  (95 shorter events, 66.8 us)
Async XLA Ops:
  7.2 214.4 %all-gather.5.cloned.1.call-start = ((), (), s32[]{:S(2)}) async-start(), calls=%async_computation.5 | async-start | bytes 15728640 | tf_op jit(solution)/shard_map/all_gather | solution.py:61
  7.2 72.3 %collective-permute-start.1 = (bf16[1,1,2,1024,768]{4,3,2,1,0:T(8,128)(2,1)}, bf16[1,1,2,1024,768]{4,3,2,1,0:T(8,128)(2,1)S(1)}, u32[]{:S(2)}, u32[]{:S(2)}) collective-permute-start(bf16[1,1,2,1024,768]{4,3,2,1,0:T(8,128)(2,1)} %param.13), channel_id=1, source_target_pairs={{0,32},{4,36},{8,40},{12,44},{16,48},{20,52},{24,56},{28,60},{32,0... | collective-permute-start | bytes 9437192 | tf_op jit(solution)/shard_map/ppermute | solution.py:12
  79.5 6.1 copy-start.8
  79.5 6.5 copy-start
  82.2 17.1 %copy-start.5 = (bf16[2,64,4096]{2,1,0:T(8,128)(2,1)S(1)}, bf16[2,64,4096]{2,1,0:T(8,128)(2,1)}, u32[]{:S(2)}) copy-start(bf16[2,64,4096]{2,1,0:T(8,128)(2,1)} %param.10) | copy-start | bytes 3145732
  82.2 39.0 %copy-start.2 = (bf16[1,1,192,4096]{3,2,1,0:T(8,128)(2,1)S(1)}, bf16[1,1,192,4096]{3,2,1,0:T(8,128)(2,1)}, u32[]{:S(2)}) copy-start(bf16[1,1,192,4096]{3,2,1,0:T(8,128)(2,1)} %param.14) | copy-start | bytes 4718596
  82.2 191.3 %all-gather.3.cloned.1.call-start = ((), (), s32[]{:S(2)}) async-start(), calls=%async_computation.4 | async-start | bytes 7864320 | tf_op jit(solution)/shard_map/all_gather | solution.py:62
  82.3 39.0 %collective-permute-start = (bf16[1,1,192,4096]{3,2,1,0:T(8,128)(2,1)}, bf16[1,1,192,4096]{3,2,1,0:T(8,128)(2,1)}, u32[]{:S(2)}, u32[]{:S(2)}) collective-permute-start(bf16[1,1,192,4096]{3,2,1,0:T(8,128)(2,1)} %param.14), channel_id=1, source_target_pairs={{0,32},{4,36},{8,40},{12,44},{16,48},{20,52},{24,56},{28,60},{32,0... | collective-permute-start | bytes 4718600 | tf_op jit(solution)/shard_map/ppermute | solution.py:12
  86.6 38.1 %copy-start.6 = (f32[1,4096]{1,0:T(1,128)S(1)}, f32[1,4096]{1,0:T(1,128)}, u32[]{:S(2)}) copy-start(f32[1,4096]{1,0:T(1,128)} %param.12) | copy-start | bytes 49156
  221.6 8.2 %copy-start.1 = (bf16[16,1,36,4096]{3,2,1,0:T(8,128)(2,1)S(1)}, bf16[16,1,36,4096]{3,2,1,0:T(8,128)(2,1)}, u32[]{:S(2)}) copy-start(bf16[16,1,36,4096]{3,2,1,0:T(8,128)(2,1)} %all_to_all.20) | copy-start | bytes 14155780
  221.6 9.7 %copy-start.9 = (bf16[1,1,2,4096,768]{4,3,2,1,0:T(8,128)(2,1)S(1)}, bf16[1,1,2,4096,768]{4,3,2,1,0:T(8,128)(2,1)}, u32[]{:S(2)}) copy-start(bf16[1,1,2,4096,768]{4,3,2,1,0:T(8,128)(2,1)} %all-gather.5.cloned.1.call-done) | copy-start | bytes 37748740
  282.3 6.8 %copy-start.7 = (f32[1,2,64,8]{2,3,1,0:T(8,128)S(1)}, f32[1,2,64,8]{2,3,1,0:T(8,128)}, u32[]{:S(2)}) copy-start(f32[1,2,64,8]{2,3,1,0:T(8,128)} %param.18) | copy-start | bytes 12292
  282.3 69.8 %all-to-all-start.1 = ((bf16[16,1,36,4096]{3,2,1,0:T(8,128)(2,1)}), bf16[16,1,36,4096]{3,2,1,0:T(8,128)(2,1)}, u32[]{:S(2)}, u32[]{:S(2)}) async-start(bf16[16,1,36,4096]{3,2,1,0:T(8,128)(2,1)} %fusion.4), calls=%async_computation.1 | async-start | bytes 10485760 | tf_op jit(solution)/shard_map/all_to_all | solution.py:79
  376.6 15.3 %collective-permute-start.2 = (bf16[64,4096]{1,0:T(8,128)(2,1)S(1)}, bf16[64,4096]{1,0:T(8,128)(2,1)S(1)}, u32[]{:S(2)}, u32[]{:S(2)}) collective-permute-start(bf16[64,4096]{1,0:T(8,128)(2,1)S(1)} %fusion.45), channel_id=1, source_target_pairs={{0,64},{1,65},{2,66},{3,67},{4,68},{5,69},{6,70},{7,71},{8,72},{9,... | collective-permute-start | bytes 1572872 | tf_op jit(solution)/shard_map/ppermute | solution.py:18
  421.0 74.3 %slice-start = ((s8[12582912]{0:T(1024)(128)(4,1)}), s8[4194304]{0:T(1024)(128)(4,1)S(1)}, s32[]{:S(2)}) async-start(s8[12582912]{0:T(1024)(128)(4,1)} %bitcast.223), calls=%async_computation.6 | async-start | bytes 8388608
  488.4 7.0 %slice-start.1 = ((s8[12582912]{0:T(1024)(128)(4,1)}), s8[4194304]{0:T(1024)(128)(4,1)S(1)}, s32[]{:S(2)}) async-start(s8[12582912]{0:T(1024)(128)(4,1)} %bitcast.223), calls=%async_computation.7 | async-start | bytes 8388608
  488.4 7.0 %slice-start.2 = ((s8[12582912]{0:T(1024)(128)(4,1)}), s8[4194304]{0:T(1024)(128)(4,1)S(1)}, s32[]{:S(2)}) async-start(s8[12582912]{0:T(1024)(128)(4,1)} %bitcast.223), calls=%async_computation.8 | async-start | bytes 8388608
  508.8 4.7 copy-start.3
  508.8 136.4 %all-to-all-start.3 = ((bf16[16,1,36,4096]{3,2,1,0:T(8,128)(2,1)}), bf16[16,1,36,4096]{3,2,1,0:T(8,128)(2,1)}, u32[]{:S(2)}, u32[]{:S(2)}) async-start(bf16[16,1,36,4096]{3,2,1,0:T(8,128)(2,1)} %fusion.7), calls=%async_computation.3 | async-start | bytes 10485760 | tf_op jit(solution)/shard_map/all_to_all | solution.py:79
  513.5 95.0 %collective-permute-start.4 = (bf16[1,1,192,4096]{3,2,1,0:T(8,128)(2,1)S(1)}, bf16[1,1,192,4096]{3,2,1,0:T(8,128)(2,1)}, u32[]{:S(2)}, u32[]{:S(2)}) collective-permute-start(bf16[1,1,192,4096]{3,2,1,0:T(8,128)(2,1)S(1)} %copy-done.3), channel_id=1, source_target_pairs={{0,32},{4,36},{8,40},{12,44},{16,48},{20,52},{24,56},{28,60},{32,0... | collective-permute-start | bytes 4718600 | tf_op jit(solution)/shard_map/ppermute | solution.py:12
  516.9 124.9 %collective-permute-start.3 = (bf16[1,1,192,4096]{3,2,1,0:T(8,128)(2,1)}, bf16[1,1,192,4096]{3,2,1,0:T(8,128)(2,1)}, u32[]{:S(2)}, u32[]{:S(2)}) collective-permute-start(bf16[1,1,192,4096]{3,2,1,0:T(8,128)(2,1)} %param.15), channel_id=1, source_target_pairs={{0,32},{4,36},{8,40},{12,44},{16,48},{20,52},{24,56},{28,60},{32,0... | collective-permute-start | bytes 4718600 | tf_op jit(solution)/shard_map/ppermute | solution.py:12
  517.4 124.4 %copy-start.4 = (bf16[1,1,192,4096]{3,2,1,0:T(8,128)(2,1)S(1)}, bf16[1,1,192,4096]{3,2,1,0:T(8,128)(2,1)}, u32[]{:S(2)}) copy-start(bf16[1,1,192,4096]{3,2,1,0:T(8,128)(2,1)} %param.15) | copy-start | bytes 4718596
Sparse Core Ops, SparseCore 0:
  82.3 122.2 all-gather.4
  206.8 66.6 all-gather.2
where the time goes:
time: 689 us; the launch traced here: 678 us
  waiting for transfers between devices  315 us (46%)
  blocking collectives  135 us (20%)
  local copies, waits for them, and re-layouts  98.9 us (14%)
  other arithmetic  47.6 us (7%)
  matrix products  42 us (6%)
  starting transfers between devices  23.9 us (3%)
  between operations  14.5 us (2%)
    ppermute x4, waiting for transfers between devices, partner(): lax.ppermute(value, axis, [(i, i ^ 1 << bit) for i in range(lax.axis_size...  209 us
    all_to_all x2, blocking collectives, layer(): lax.all_to_all(outgoing, 'expert', split_axis=0, concat_axis=0, tiled=True)  135 us
    all_to_all x2, waiting for transfers between devices, expert_work(): lax.all_to_all(result, 'expert', split_axis=0, concat_axis=0, tiled=True)  61.3 us
    scatter x2, local copies, waits for them, and re-layouts, layer(): outgoing = outgoing.at[position].set(normed[token_rows])  42.7 us
    all_gather x1, waiting for transfers between devices, per_device(): lax.all_gather(local_down, 'dp', axis=2, tiled=True)  37.7 us
    gather x2, local copies, waits for them, and re-layouts, layer(): rows_back = returned.reshape(-1, width)[position].astype(jnp.float32)  23 us
    dot_general x2, matrix products, expert_work(): jnp.einsum('sicf,ifd->sicd', active, down_weights, preferred_element_type...  17.6 us
    dot_general x2, matrix products, expert_work(): jnp.einsum('sicd,idf->sicf', arrived, gate_weights, preferred_element_typ...  15.2 us
  transfers between devices with their start and end apart: 9, of which 7 were waited for; matrix products, arithmetic and copies ran while one was open for 11% of the time, Pallas kernels for 0%

commit v1 on v0

v1 whole, which is shorter than its diff:
```python
import jax
import jax.numpy as jnp
from jax import lax
from jax.sharding import PartitionSpec as P

EXPERTS = 16


def partner(value, axis, bit):
    return lax.ppermute(value, axis, [(i, i ^ 1 << bit) for i in range(lax.axis_size(axis))])


def shifted(block, axis, distance):
    devices = range(lax.axis_size(axis))
    route = [(i - distance, i) for i in devices if i - distance in devices]
    return lax.ppermute(block, axis, route)


def rms_normed(inputs, norm_gain):
    values = inputs.astype(jnp.float32)
    inverse_rms = lax.rsqrt(jnp.mean(values * values, axis=-1, keepdims=True) + 1e-06)
    return (values * inverse_rms * norm_gain).astype(jnp.bfloat16)


def per_device(
    fresh_tokens,
    in_flight,
    norm_weight,
    gate_up,
    down_proj,
    first_moment,
    second_moment,
    route_ids,
    route_probs,
    trade_flags,
):
    groups = lax.axis_size("expert")
    half_span = groups // 2
    top_bit = groups.bit_length() - 2
    own_rank = lax.axis_index("expert")
    section_index = lax.axis_index("section")
    full_gate_up = lax.all_gather(gate_up, "dp", axis=3, tiled=True)
    full_down = lax.all_gather(down_proj, "dp", axis=2, tiled=True)
    gate_weights = full_gate_up[0, 0, 0]
    up_weights = full_gate_up[0, 0, 1]
    down_weights = full_down[0, 0]
    expert_ids = jnp.arange(EXPERTS, dtype=jnp.int32)
    probs = route_probs[0]
    mix = probs / jnp.sum(probs, axis=-1, keepdims=True)
    chosen = route_ids[0][:, :, :, None] == expert_ids
    dense_mix = jnp.sum(jnp.where(chosen, mix[:, :, :, None], 0.0), axis=2)
    all_mix = lax.all_gather(dense_mix, "expert", axis=1, tiled=True)
    own_mix = jnp.sum(jnp.where(expert_ids == own_rank, all_mix, 0.0), axis=-1)

    traded = partner((gate_up, down_proj, first_moment, second_moment), "expert", top_bit)

    def layer(inputs, scale, held=None):
        normed = rms_normed(inputs, norm_weight[0])
        arrived = lax.all_gather(normed, "expert", axis=0, tiled=True)
        gate_part = jnp.dot(arrived, gate_weights, preferred_element_type=jnp.float32)
        up_part = jnp.dot(arrived, up_weights, preferred_element_type=jnp.float32)
        active = (jax.nn.silu(gate_part) * up_part).astype(jnp.bfloat16)
        result = jnp.dot(active, down_weights, preferred_element_type=jnp.float32)
        result = (result * scale[:, None]).astype(jnp.bfloat16)
        if held is not None:
            result, held = lax.optimization_barrier((result, held))
        combined = lax.psum_scatter(result, "expert", scatter_dimension=0, tiled=True)
        return (inputs.astype(jnp.float32) + combined.astype(jnp.float32)).astype(jnp.bfloat16), held

    first_input = jnp.where(section_index == 0, fresh_tokens[0], in_flight)
    tick_zero, traded = layer(first_input, own_mix[0], traded)
    arrived = shifted(tick_zero, "section", 1)
    second_input = jnp.where(section_index == 0, fresh_tokens[1], arrived)
    tick_one, _ = layer(second_input, own_mix[1])
    layer_out = jnp.stack([tick_zero, tick_one])[None]

    own_flags = trade_flags[own_rank % half_span] == 1
    mask_five = own_flags[None, :, None, None, None]
    mask_four = own_flags[None, :, None, None]
    gate_up_moved = jnp.where(mask_five, traded[0], gate_up)
    down_moved = jnp.where(mask_four, traded[1], down_proj)
    first_moved = jnp.where(mask_four, traded[2], first_moment)
    second_moved = jnp.where(mask_four, traded[3], second_moment)
    return (layer_out, gate_up_moved, down_moved, first_moved, second_moved)


def solution(mesh):
    return jax.shard_map(
        per_device,
        mesh=mesh,
        in_specs=(
            P(None, ("expert", "dp"), None),
            P(("expert", "dp"), None),
            P("section", None),
            P("section", "expert", None, "dp", None),
            P("section", "expert", "dp", None),
            P("section", "expert", "dp", None),
            P("section", "expert", "dp", None),
            P("section", None, ("expert", "dp"), None),
            P("section", None, ("expert", "dp"), None),
            P(),
        ),
        out_specs=(
            P("section", None, ("expert", "dp"), None),
            P("section", "expert", None, "dp", None),
            P("section", "expert", "dp", None),
            P("section", "expert", "dp", None),
            P("section", "expert", "dp", None),
        ),
        check_vma=False,
    )
```

time: 689 us -> 781 us (1.13); the launches traced: 678 us -> 779 us
  waiting for transfers between devices: 315 us -> 633 us
  blocking collectives: 135 us -> 34.4 us
  local copies, waits for them, and re-layouts: 98.9 us -> 6.05 us
  other arithmetic: 47.6 us -> 18.7 us
  matrix products: 42 us -> 62.9 us
  starting transfers between devices: 23.9 us -> 9.3 us
    all_gather x2 -> x4, waiting for transfers between devices: 37.7 us -> 425 us  [the longest x2 257 us: layer(): arrived = lax.all_gather(normed, 'expert', axis=0, tiled=True)]
    ppermute x4, waiting for transfers between devices: 209 us -> 0.01 us  [partner(): lax.ppermute(value, axis, [(i, i ^ 1 << bit) for i in range(lax.axis_size...]
    reduce_scatter x0 -> x2, waiting for transfers between devices: none -> 194 us  [layer(): lax.psum_scatter(result, 'expert', scatter_dimension=0, tiled=True)]
    all_to_all x2 -> x0, blocking collectives: 135 us -> none  [layer(): lax.all_to_all(outgoing, 'expert', split_axis=0, concat_axis=0, tiled=True)]
    all_to_all x2 -> x0, waiting for transfers between devices: 61.3 us -> none  [expert_work(): lax.all_to_all(result, 'expert', split_axis=0, concat_axis=0, tiled=True)]
    scatter x2 -> x0, local copies, waits for them, and re-layouts: 42.7 us -> none  [layer(): outgoing = outgoing.at[position].set(normed[token_rows])]
    all_gather x0 -> x1, blocking collectives: none -> 34.4 us  [per_device(): all_mix = lax.all_gather(dense_mix, 'expert', axis=1, tiled=True)]
    reshape x4 -> x0, local copies, waits for them, and re-layouts: 29 us -> none  [the longest x2 14.5 us: layer(): rows_back = returned.reshape(-1, width)[position].astype(jnp.float32)]
  transfers between devices with their start and end apart: 9 -> 11, of which waited for: 7 -> 7; matrix products, arithmetic and copies ran while one was open for 11% -> 6% of each run, Pallas kernels for 0% -> 0%
where the time goes in v1:
time: 781 us; the launch traced here: 779 us
  waiting for transfers between devices  633 us (81%)
  matrix products  62.9 us (8%)
  blocking collectives  34.4 us (4%)
  other arithmetic  18.7 us (2%)
  between operations  14.3 us (2%)
  starting transfers between devices  9.3 us (1%)
    all_gather x2, waiting for transfers between devices, layer(): arrived = lax.all_gather(normed, 'expert', axis=0, tiled=True)  257 us
    reduce_scatter x2, waiting for transfers between devices, layer(): lax.psum_scatter(result, 'expert', scatter_dimension=0, tiled=True)  194 us
    all_gather x1, waiting for transfers between devices, per_device(): full_gate_up = lax.all_gather(gate_up, 'dp', axis=3, tiled=True)  119 us
    all_gather x1, waiting for transfers between devices, per_device(): full_down = lax.all_gather(down_proj, 'dp', axis=2, tiled=True)  49.1 us
    all_gather x1, blocking collectives, per_device(): all_mix = lax.all_gather(dense_mix, 'expert', axis=1, tiled=True)  34.4 us
    dot_general x2, matrix products, layer(): result = jnp.dot(active, down_weights, preferred_element_type=jnp.float32)  23 us
    dot_general x2, matrix products, layer(): up_part = jnp.dot(arrived, up_weights, preferred_element_type=jnp.float32)  22.1 us
    dot_general x2, matrix products, layer(): jnp.dot(arrived, gate_weights, preferred_element_type=jnp.float32)  17.8 us
  transfers between devices with their start and end apart: 11, of which 7 were waited for; matrix products, arithmetic and copies ran while one was open for 6% of the time, Pallas kernels for 0%

profile of v1, /device:TPU:2, one launch (start us, length us, event | category | flops | bytes accessed | tf_op | source)
XLA Modules:
  0.0 779.1 jit_solution(14578231850789856475)
XLA Ops:
  7.2 1.5 fusion.6
  9.5 1.8 fusion.8
  12.9 4.0 collective-permute-start.1
  17.0 3.4 collective-permute-start.2
  20.7 34.4 %all_gather.18 = f32[2,1024,16]{2,0,1:T(2,128)S(1)} all-gather(f32[2,64,16]{2,0,1:T(2,128)S(1)} %copy.17), channel_id=1, replica_groups=mesh['section'=2,'expert'=16,'dp'=4] {'expert'}, dimensions={1}, use_global_device_ids=true | all-gather | bytes 139264 | tf_op jit(solution)/shard_map/all_gather | solution.py:52
  58.6 187.4 %all-gather.5.cloned.1.call-done = bf16[1024,4096]{1,0:T(8,128)(2,1)} async-done(((bf16[64,4096]{1,0:T(8,128)(2,1)}), bf16[1024,4096]{1,0:T(8,128)(2,1)}) %all-gather.5.cloned.1.call-update) | async-done | bytes 8388624 | tf_op jit(solution)/shard_map/all_gather | solution.py:59
  246.0 118.9 %all-gather.7.cloned.1.call-done = bf16[1,1,2,4096,768]{4,3,2,1,0:T(8,128)(2,1)} async-done(((bf16[1,1,2,1024,768]{4,3,2,1,0:T(8,128)(2,1)}), bf16[1,1,2,4096,768]{4,3,2,1,0:T(8,128)(2,1)}) %all-gather.7.cloned.1.call-update) | async-done | bytes 12582928 | tf_op jit(solution)/shard_map/all_gather | solution.py:42
  364.9 11.0 %fusion.5 = f32[1024,768]{1,0:T(8,128)S(1)} fusion(bf16[1024,4096]{1,0:T(8,128)(2,1)} %all-gather.5.cloned.1.call-done, bf16[1,1,2,4096,768]{4,3,2,1,0:T(8,128)(2,1)} %all-gather.7.cloned.1.call-done), kind=kOutput, calls=%fused_computation.9 | convolution fusion | flops 6442450944 | bytes 17825792 | tf_op jit(solution)/shard_map/dot_general | solution.py:61
  376.1 8.1 %multiply_convert_fusion.3 = bf16[1024,768]{1,0:T(8,128)(2,1)} fusion(f32[1024,768]{1,0:T(8,128)S(1)} %fusion.5, bf16[1024,4096]{1,0:T(8,128)(2,1)S(1)} %copy-done.13, bf16[1,1,2,4096,768]{4,3,2,1,0:T(8,128)(2,1)S(1)} %copy-done.12), kind=kOutput, calls=%fused_computation.11 | convolution fusion | flops 6447169536 | bytes 19398656 | tf_op jit(solution)/shard_map/dot_general | solution.py:60
  384.1 49.1 %all-gather.9.cloned.1.call-done = bf16[1,1,768,4096]{3,2,1,0:T(8,128)(2,1)} async-done(((bf16[1,1,192,4096]{3,2,1,0:T(8,128)(2,1)}), bf16[1,1,768,4096]{3,2,1,0:T(8,128)(2,1)}) %all-gather.9.cloned.1.call-update) | async-done | bytes 6291472 | tf_op jit(solution)/shard_map/all_gather | solution.py:43
  433.3 11.2 %multiply_convert_fusion.1 = bf16[1024,4096]{1,0:T(8,128)(2,1)} fusion(f32[1024]{0:T(1024)S(1)} %bitcast.45, bf16[1024,768]{1,0:T(8,128)(2,1)} %multiply_convert_fusion.3, bf16[1,1,768,4096]{3,2,1,0:T(8,128)(2,1)} %all-gather.9.cloned.1.call-done), kind=kOutput, calls=%fused_computation.1 | convolution fusion | flops 6450839552 | bytes 16257024 | tf_op jit(solution)/shard_map/dot_general | solution.py:63
  444.6 102.3 %reduce-scatter.3.cloned.1.call-done = bf16[64,4096]{1,0:T(8,128)(2,1)} async-done(((bf16[1024,4096]{1,0:T(8,128)(2,1)}), bf16[64,4096]{1,0:T(8,128)(2,1)}) %reduce-scatter.3.cloned.1.call-update) | async-done | bytes 524304 | tf_op jit(solution)/shard_map/reduce_scatter | solution.py:67
  546.9 1.3 fusion.9
  548.3 1.3 collective-permute-start.4
  549.6 13.2 %collective-permute-done.4 = bf16[64,4096]{1,0:T(8,128)(2,1)S(1)} collective-permute-done((bf16[64,4096]{1,0:T(8,128)(2,1)S(1)}, bf16[64,4096]{1,0:T(8,128)(2,1)S(1)}, u32[]{:S(2)}, u32[]{:S(2)}) %collective-permute-start.4) | collective-permute-done | bytes 524320 | tf_op jit(solution)/shard_map/ppermute | solution.py:16
  562.8 1.3 fusion.10
  567.4 69.7 %all-gather.11.cloned.1.call-done = bf16[1024,4096]{1,0:T(8,128)(2,1)} async-done(((bf16[64,4096]{1,0:T(8,128)(2,1)}), bf16[1024,4096]{1,0:T(8,128)(2,1)}) %all-gather.11.cloned.1.call-update) | async-done | bytes 8388624 | tf_op jit(solution)/shard_map/all_gather | solution.py:59
  637.1 11.0 %fusion.4 = f32[1024,768]{1,0:T(8,128)S(1)} fusion(bf16[1024,4096]{1,0:T(8,128)(2,1)} %all-gather.11.cloned.1.call-done, bf16[1,1,2,4096,768]{4,3,2,1,0:T(8,128)(2,1)} %all-gather.7.cloned.1.call-done), kind=kOutput, calls=%fused_computation.8 | convolution fusion | flops 6442450944 | bytes 17825792 | tf_op jit(solution)/shard_map/dot_general | solution.py:61
  648.1 9.8 %multiply_convert_fusion.2 = bf16[1024,768]{1,0:T(8,128)(2,1)S(1)} fusion(f32[1024,768]{1,0:T(8,128)S(1)} %fusion.4, bf16[1024,4096]{1,0:T(8,128)(2,1)S(1)} %copy-done.14, bf16[1,1,2,4096,768]{4,3,2,1,0:T(8,128)(2,1)} %all-gather.7.cloned.1.call-done), kind=kOutput, calls=%fused_computation.10 | convolution fusion | flops 6447169536 | bytes 19398656 | tf_op jit(solution)/shard_map/dot_general | solution.py:60
  657.9 11.7 %multiply_convert_fusion = bf16[1024,4096]{1,0:T(8,128)(2,1)} fusion(f32[1024]{0:T(1024)S(1)} %bitcast.46, bf16[1024,768]{1,0:T(8,128)(2,1)S(1)} %multiply_convert_fusion.2, bf16[1,1,768,4096]{3,2,1,0:T(8,128)(2,1)} %all-gather.9.cloned.1.call-done), kind=kOutput, calls=%fused_computation | convolution fusion | flops 6450839552 | bytes 16257024 | tf_op jit(solution)/shard_map/dot_general | solution.py:63
  670.9 2.8 broadcast_select_fusion
  673.7 2.2 broadcast_select_fusion.3
  675.8 2.7 broadcast_select_fusion.1
  678.5 91.4 %reduce-scatter.5.cloned.1.call-done = bf16[64,4096]{1,0:T(8,128)(2,1)} async-done(((bf16[1024,4096]{1,0:T(8,128)(2,1)}), bf16[64,4096]{1,0:T(8,128)(2,1)}) %reduce-scatter.5.cloned.1.call-update) | async-done | bytes 524304 | tf_op jit(solution)/shard_map/reduce_scatter | solution.py:67
  (65 shorter events, 13.1 us)
Async XLA Ops:
  7.2 238.8 %all-gather.5.cloned.1.call-start = ((), (), s32[]{:S(2)}) async-start(), calls=%async_computation.2 | async-start | bytes 8912896 | tf_op jit(solution)/shard_map/all_gather | solution.py:59
  9.5 7.4 copy-start
  9.5 11.0 %copy-start.10 = (f32[1,2,64,8]{2,3,1,0:T(8,128)S(1)}, f32[1,2,64,8]{2,3,1,0:T(8,128)}, u32[]{:S(2)}) copy-start(f32[1,2,64,8]{2,3,1,0:T(8,128)} %param.18) | copy-start | bytes 12292
  9.5 11.0 %copy-start.11 = (s32[1,2,64,8]{2,3,1,0:T(8,128)S(1)}, s32[1,2,64,8]{2,3,1,0:T(8,128)}, u32[]{:S(2)}) copy-start(s32[1,2,64,8]{2,3,1,0:T(8,128)} %param.17) | copy-start | bytes 12292
  11.4 353.5 %all-gather.7.cloned.1.call-start = ((), (), s32[]{:S(2)}) async-start(), calls=%async_computation.3 | async-start | bytes 15728640 | tf_op jit(solution)/shard_map/all_gather | solution.py:42
  12.1 421.1 %all-gather.9.cloned.1.call-start = ((), (), s32[]{:S(2)}) async-start(), calls=%async_computation.4 | async-start | bytes 7864320 | tf_op jit(solution)/shard_map/all_gather | solution.py:43
  12.9 534.1 %reduce-scatter.3.cloned.1.call-start = ((), (), s32[]{:S(2)}) async-start(), calls=%async_computation.5 | async-start | bytes 8912896 | tf_op jit(solution)/shard_map/reduce_scatter | solution.py:67
  12.9 431.6 %collective-permute-start.1 = (bf16[1,1,192,4096]{3,2,1,0:T(8,128)(2,1)}, bf16[1,1,192,4096]{3,2,1,0:T(8,128)(2,1)}, u32[]{:S(2)}, u32[]{:S(2)}) collective-permute-start(bf16[1,1,192,4096]{3,2,1,0:T(8,128)(2,1)} %param.14), channel_id=1, source_target_pairs={{0,32},{4,36},{8,40},{12,44},{16,48},{20,52},{24,56},{28,60},{32,0... | collective-permute-start | bytes 4718600 | tf_op jit(solution)/shard_map/ppermute | solution.py:10
  16.9 427.6 %collective-permute-start = (bf16[1,1,2,1024,768]{4,3,2,1,0:T(8,128)(2,1)S(1)}, bf16[1,1,2,1024,768]{4,3,2,1,0:T(8,128)(2,1)}, u32[]{:S(2)}, u32[]{:S(2)}) collective-permute-start(bf16[1,1,2,1024,768]{4,3,2,1,0:T(8,128)(2,1)S(1)} %copy-done), channel_id=1, source_target_pairs={{0,32},{4,36},{8,40},{12,44},{16,48},{20,52},{24,56},{28,60},{32,0... | collective-permute-start | bytes 9437192 | tf_op jit(solution)/shard_map/ppermute | solution.py:10
  17.0 427.5 %collective-permute-start.2 = (bf16[1,1,192,4096]{3,2,1,0:T(8,128)(2,1)}, bf16[1,1,192,4096]{3,2,1,0:T(8,128)(2,1)}, u32[]{:S(2)}, u32[]{:S(2)}) collective-permute-start(bf16[1,1,192,4096]{3,2,1,0:T(8,128)(2,1)} %param.15), channel_id=1, source_target_pairs={{0,32},{4,36},{8,40},{12,44},{16,48},{20,52},{24,56},{28,60},{32,0... | collective-permute-start | bytes 4718600 | tf_op jit(solution)/shard_map/ppermute | solution.py:10
  20.4 424.1 %collective-permute-start.3 = (bf16[1,1,192,4096]{3,2,1,0:T(8,128)(2,1)}, bf16[1,1,192,4096]{3,2,1,0:T(8,128)(2,1)}, u32[]{:S(2)}, u32[]{:S(2)}) collective-permute-start(bf16[1,1,192,4096]{3,2,1,0:T(8,128)(2,1)} %param.16), channel_id=1, source_target_pairs={{0,32},{4,36},{8,40},{12,44},{16,48},{20,52},{24,56},{28,60},{32,0... | collective-permute-start | bytes 4718600 | tf_op jit(solution)/shard_map/ppermute | solution.py:10
  364.9 11.0 %copy-start.12 = (bf16[1,1,2,4096,768]{4,3,2,1,0:T(8,128)(2,1)S(1)}, bf16[1,1,2,4096,768]{4,3,2,1,0:T(8,128)(2,1)}, u32[]{:S(2)}) copy-start(bf16[1,1,2,4096,768]{4,3,2,1,0:T(8,128)(2,1)} %all-gather.7.cloned.1.call-done) | copy-start | bytes 37748740
  364.9 11.2 %copy-start.13 = (bf16[1024,4096]{1,0:T(8,128)(2,1)S(1)}, bf16[1024,4096]{1,0:T(8,128)(2,1)}, u32[]{:S(2)}) copy-start(bf16[1024,4096]{1,0:T(8,128)(2,1)} %all-gather.5.cloned.1.call-done) | copy-start | bytes 25165828
  444.6 120.4 %copy-start.9 = (f32[1,4096]{1,0:T(1,128)S(1)}, f32[1,4096]{1,0:T(1,128)}, u32[]{:S(2)}) copy-start(f32[1,4096]{1,0:T(1,128)} %param.12) | copy-start | bytes 49156
  444.6 192.5 %all-gather.11.cloned.1.call-start = ((), (), s32[]{:S(2)}) async-start(), calls=%async_computation.6 | async-start | bytes 8912896 | tf_op jit(solution)/shard_map/all_gather | solution.py:59
  548.3 1.3 copy-start.5
  548.3 14.5 %collective-permute-start.4 = (bf16[64,4096]{1,0:T(8,128)(2,1)S(1)}, bf16[64,4096]{1,0:T(8,128)(2,1)S(1)}, u32[]{:S(2)}, u32[]{:S(2)}) collective-permute-start(bf16[64,4096]{1,0:T(8,128)(2,1)S(1)} %fusion.9), channel_id=1, source_target_pairs={{0,64},{1,65},{2,66},{3,67},{4,68},{5,69},{6,70},{7,71},{8,72},{9,... | collective-permute-start | bytes 1572872 | tf_op jit(solution)/shard_map/ppermute | solution.py:16
  565.9 204.1 %reduce-scatter.5.cloned.1.call-start = ((), (), s32[]{:S(2)}) async-start(), calls=%async_computation.7 | async-start | bytes 8912896 | tf_op jit(solution)/shard_map/reduce_scatter | solution.py:67
  637.1 11.0 %copy-start.14 = (bf16[1024,4096]{1,0:T(8,128)(2,1)S(1)}, bf16[1024,4096]{1,0:T(8,128)(2,1)}, u32[]{:S(2)}) copy-start(bf16[1024,4096]{1,0:T(8,128)(2,1)} %all-gather.11.cloned.1.call-done) | copy-start | bytes 25165828
  670.9 2.8 copy-start.1
  673.6 2.2 copy-start.7
  673.7 2.2 copy-start.8
  675.8 94.2 %copy-start.4 = (bf16[64,4096]{1,0:T(8,128)(2,1)S(1)}, bf16[64,4096]{1,0:T(8,128)(2,1)}, u32[]{:S(2)}) copy-start(bf16[64,4096]{1,0:T(8,128)(2,1)} %copy-done.3) | copy-start | bytes 1572868
  675.8 95.4 %copy-start.6 = (bf16[64,4096]{1,0:T(8,128)(2,1)S(1)}, bf16[64,4096]{1,0:T(8,128)(2,1)}, u32[]{:S(2)}) copy-start(bf16[64,4096]{1,0:T(8,128)(2,1)} %copy-done.5) | copy-start | bytes 1572868
  (3 other events, 2.3 us)
Sparse Core Ops, SparseCore 0:
  11.5 234.3 all-gather.4
  247.6 117.1 all-gather.6
  366.5 66.6 all-gather.8
  444.7 102.2 reduce-scatter.2
  566.1 70.9 all-gather.10
  669.8 100.1 reduce-scatter.4

commit v2 on v1

v2 whole, which is shorter than its diff:
```python
import jax
import jax.numpy as jnp
from jax import lax
from jax.experimental import pallas as pl
from jax.experimental.pallas import tpu as pltpu
from jax.sharding import PartitionSpec as P

EXPERTS = 16
MESH = pl.DeviceIdType.MESH
ANY = pl.BlockSpec(memory_space=pl.ANY)
VMEM = pl.BlockSpec(memory_space=pltpu.VMEM)
DMA = pltpu.SemaphoreType.DMA
CHIPS = [(dz, dx) for dz in (1, 3, 2, 0) for dx in (0, 1) if dz or dx]


def chip_peer(rank, dz, dx):
    return lax.rem(rank + 4 * dz, EXPERTS) ^ (2 * dx)


def remote(src, dst, send_sem, recv_sem, **device):
    return pltpu.make_async_remote_copy(
        src_ref=src,
        dst_ref=dst,
        send_sem=send_sem,
        recv_sem=recv_sem,
        device_id=device,
        device_id_type=MESH,
    )


def greet(devices):
    barrier = pltpu.get_barrier_semaphore()
    for device in devices:
        pl.semaphore_signal(barrier, inc=1, device_id=device, device_id_type=MESH)
    pl.semaphore_wait(barrier, len(devices))


def block(ref, rank, rows):
    return ref.at[pl.ds(pl.multiple_of(rank * rows, rows), rows)]


def gather_start(pairs, sems, rank):
    send, recv = sems
    local, first = [], []
    for k, (own, whole) in enumerate(pairs):
        rows = own.shape[0]
        here = pltpu.make_async_copy(own, block(whole, rank, rows), send.at[k, 15])
        here.start()
        local.append(here)
        for i, (dz, dx) in enumerate(CHIPS):
            copy = remote(
                own, block(whole, rank, rows), send.at[k, i], recv.at[k, i],
                expert=chip_peer(rank, dz, dx),
            )
            copy.start()
            first.append(copy)
        copy = remote(own, block(whole, rank, rows), send.at[k, 14], recv.at[k, 14], expert=rank ^ 1)
        copy.start()
        first.append(copy)
    return local, first


def gather_finish(pairs, sems, rank, started):
    send, recv = sems
    local, first = started
    second = []
    for i, (dz, dx) in enumerate(CHIPS):
        source = chip_peer(rank, (4 - dz) % 4, dx)
        for k, (own, whole) in enumerate(pairs):
            rows = own.shape[0]
            first[k * 8 + i].wait_recv()
            landed = block(whole, source, rows)
            copy = remote(landed, landed, send.at[k, 7 + i], recv.at[k, 7 + i], expert=rank ^ 1)
            copy.start()
            second.append(copy)
    for k in range(len(pairs)):
        first[k * 8 + 7].wait_recv()
    for copy in second:
        copy.wait_recv()
    for copy in first + second:
        copy.wait_send()
    for copy in local:
        copy.wait()


def group(rank):
    return [{"expert": chip_peer(rank, dz, dx)} for dz, dx in CHIPS] + [{"expert": rank ^ 1}]


def weights_kernel(gate_up, down, tokens, mix, full_gate_up, full_down, all_tokens, all_mix,
                   send, recv, here, token_send, token_recv):
    rank, place = lax.axis_index("expert"), lax.axis_index("dp")
    right, left = lax.rem(place + 1, 4), lax.rem(place + 3, 4)
    greet([{"dp": right}, {"dp": left}] + group(rank))
    deep, low = gate_up.shape[1], down.shape[0]
    half = low // 2

    def gate_part(k, owner):
        return full_gate_up.at[k, pl.ds(pl.multiple_of(owner * deep, deep), deep)]

    def down_part(k, owner):
        return full_down.at[pl.ds(pl.multiple_of(owner * low + k * half, half), half)]

    own = [gate_up.at[0], gate_up.at[1], down.at[pl.ds(0, half)], down.at[pl.ds(half, half)]]
    parts = [lambda o: gate_part(0, o), lambda o: gate_part(1, o),
             lambda o: down_part(0, o), lambda o: down_part(1, o)]
    copies = []
    for k in range(4):
        copies.append((
            remote(own[k], parts[k](place), send.at[k, 0], recv.at[k, 0], dp=right),
            remote(own[k], parts[k](place), send.at[k, 1], recv.at[k, 1], dp=left),
        ))
    for k in (0, 2):
        copies[k][0].start()
        copies[k + 1][1].start()
    for k in (0, 2):
        copies[k + 1][0].start()
        copies[k][1].start()
    pairs = [(tokens, all_tokens), (mix, all_mix)]
    sems = (token_send, token_recv)
    started = gather_start(pairs, sems, rank)
    local = []
    for k in range(4):
        copy = pltpu.make_async_copy(own[k], parts[k](place), here.at[k])
        copy.start()
        local.append(copy)
    passed = []
    for k in range(4):
        way = k % 2
        owner, device = ((left, right), (right, left))[way]
        copies[k][way].wait_recv()
        copy = remote(parts[k](owner), parts[k](owner), send.at[k, 2], recv.at[k, 2], dp=device)
        copy.start()
        passed.append(copy)
    gather_finish(pairs, sems, rank, started)
    for k in range(4):
        copies[k][1 - k % 2].wait_recv()
        passed[k].wait_recv()
    for k in range(4):
        copies[k][0].wait_send()
        copies[k][1].wait_send()
        passed[k].wait_send()
        local[k].wait()


def gather_weights(gate_up, down, tokens, mix):
    width = tokens.shape[1]
    return pl.pallas_call(
        weights_kernel,
        out_shape=(
            jax.ShapeDtypeStruct((2, 4 * gate_up.shape[1], gate_up.shape[2]), jnp.bfloat16),
            jax.ShapeDtypeStruct((4 * down.shape[0], width), jnp.bfloat16),
            jax.ShapeDtypeStruct((EXPERTS * tokens.shape[0], width), jnp.bfloat16),
            jax.ShapeDtypeStruct((EXPERTS * mix.shape[0], mix.shape[1]), jnp.float32),
        ),
        in_specs=[ANY] * 4,
        out_specs=[ANY] * 4,
        scratch_shapes=[
            DMA((4, 3)), DMA((4, 3)), DMA((4,)), DMA((2, 16)), DMA((2, 16)),
        ],
        compiler_params=pltpu.CompilerParams(collective_id=0, has_side_effects=True),
        name="gather_weights",
    )(gate_up, down, tokens, mix)


def tokens_kernel(tokens, all_tokens, token_send, token_recv):
    rank = lax.axis_index("expert")
    greet(group(rank))
    pairs, sems = [(tokens, all_tokens)], (token_send, token_recv)
    gather_finish(pairs, sems, rank, gather_start(pairs, sems, rank))


def gather_tokens(tokens):
    return pl.pallas_call(
        tokens_kernel,
        out_shape=jax.ShapeDtypeStruct((EXPERTS * tokens.shape[0], tokens.shape[1]), jnp.bfloat16),
        in_specs=[ANY],
        out_specs=ANY,
        scratch_shapes=[DMA((1, 16)), DMA((1, 16))],
        compiler_params=pltpu.CompilerParams(collective_id=1, has_side_effects=True),
        name="gather_tokens",
    )(tokens)


def combine_kernel(partial, inputs, out, mine, theirs, summed, arrived, sib_send, sib_recv,
                   load, send, recv):
    rank = lax.axis_index("expert")
    rows, width = inputs.shape
    greet(group(rank))
    steps = CHIPS + [(0, 0)]
    sibling = []
    for i, (dz, dx) in enumerate(steps):
        home = chip_peer(rank, dz, dx)
        copy = remote(block(partial, home ^ 1, rows), theirs.at[i], sib_send.at[i], sib_recv.at[i],
                      expert=rank ^ 1)
        copy.start()
        sibling.append(copy)
    loads = []
    for i, (dz, dx) in enumerate(steps):
        copy = pltpu.make_async_copy(block(partial, chip_peer(rank, dz, dx), rows), mine.at[i], load.at[i])
        copy.start()
        loads.append(copy)
    copies = []
    for i, (dz, dx) in enumerate(steps):
        loads[i].wait()
        sibling[i].wait_recv()

        @pl.loop(0, rows // 16)
        def _(r):
            part = pl.ds(pl.multiple_of(r * 16, 16), 16)
            total = mine[i, part, :].astype(jnp.float32) + theirs[i, part, :].astype(jnp.float32)
            summed[i, part, :] = total.astype(jnp.bfloat16)

        if i < 7:
            copy = remote(summed.at[i], arrived.at[i], send.at[i], recv.at[i],
                          expert=chip_peer(rank, dz, dx))
            copy.start()
            copies.append(copy)
    for copy in copies:
        copy.wait_recv()

    @pl.loop(0, rows // 16)
    def _(r):
        part = pl.ds(pl.multiple_of(r * 16, 16), 16)
        total = inputs[part, :].astype(jnp.float32) + summed[7, part, :].astype(jnp.float32)
        for i in range(7):
            total = total + arrived[i, part, :].astype(jnp.float32)
        out[part, :] = total.astype(jnp.bfloat16)

    for copy in copies + sibling:
        copy.wait_send()


def combine(partial, inputs):
    rows, width = inputs.shape
    slot = pltpu.VMEM((8, rows, width), jnp.bfloat16)
    return pl.pallas_call(
        combine_kernel,
        out_shape=jax.ShapeDtypeStruct(inputs.shape, jnp.bfloat16),
        in_specs=[ANY, VMEM],
        out_specs=VMEM,
        scratch_shapes=[
            slot, slot, slot, pltpu.VMEM((7, rows, width), jnp.bfloat16),
            DMA((8,)), DMA((8,)), DMA((8,)), DMA((7,)), DMA((7,)),
        ],
        compiler_params=pltpu.CompilerParams(
            collective_id=2, has_side_effects=True, vmem_limit_bytes=40 << 20
        ),
        name="combine",
    )(partial, inputs)


def partner(value, axis, bit):
    return lax.ppermute(value, axis, [(i, i ^ 1 << bit) for i in range(lax.axis_size(axis))])


def shifted(value, axis, distance):
    devices = range(lax.axis_size(axis))
    route = [(i - distance, i) for i in devices if i - distance in devices]
    return lax.ppermute(value, axis, route)


def rms_normed(inputs, norm_gain):
    values = inputs.astype(jnp.float32)
    inverse_rms = lax.rsqrt(jnp.mean(values * values, axis=-1, keepdims=True) + 1e-06)
    return (values * inverse_rms * norm_gain).astype(jnp.bfloat16)


def expert_ffn(rows_in, gate_up, down, scale):
    gate_part = jnp.dot(rows_in, gate_up[0], preferred_element_type=jnp.float32)
    up_part = jnp.dot(rows_in, gate_up[1], preferred_element_type=jnp.float32)
    active = (jax.nn.silu(gate_part) * up_part).astype(jnp.bfloat16)
    result = jnp.dot(active, down, preferred_element_type=jnp.float32)
    return (result * scale[:, None]).astype(jnp.bfloat16)


def per_device(
    fresh_tokens,
    in_flight,
    norm_weight,
    gate_up,
    down_proj,
    first_moment,
    second_moment,
    route_ids,
    route_probs,
    trade_flags,
):
    groups = lax.axis_size("expert")
    half_span = groups // 2
    top_bit = groups.bit_length() - 2
    own_rank = lax.axis_index("expert")
    section_index = lax.axis_index("section")
    traded = partner((gate_up, down_proj, first_moment, second_moment), "expert", top_bit)

    lanes = jnp.arange(128, dtype=jnp.int32)
    probs = route_probs[0]
    mix = probs / jnp.sum(probs, axis=-1, keepdims=True)
    wanted = route_ids[0] + EXPERTS * jnp.arange(2, dtype=jnp.int32)[:, None, None]
    dense_mix = jnp.sum(jnp.where(wanted[..., None] == lanes, mix[..., None], 0.0), axis=(0, 2))

    first_input = jnp.where(section_index == 0, fresh_tokens[0], in_flight)
    full_gate_up, full_down, all_tokens, all_mix = gather_weights(
        gate_up[0, 0], down_proj[0, 0], rms_normed(first_input, norm_weight[0]), dense_mix
    )

    def own_mix(tick):
        return jnp.sum(jnp.where(lanes == tick * EXPERTS + own_rank, all_mix, 0.0), axis=-1)

    partial = expert_ffn(all_tokens, full_gate_up, full_down, own_mix(0))
    partial, traded = lax.optimization_barrier((partial, traded))
    tick_zero = combine(partial, first_input)
    arrived = shifted(tick_zero, "section", 1)
    second_input = jnp.where(section_index == 0, fresh_tokens[1], arrived)
    all_tokens = gather_tokens(rms_normed(second_input, norm_weight[0]))
    partial = expert_ffn(all_tokens, full_gate_up, full_down, own_mix(1))
    tick_one = combine(partial, second_input)
    layer_out = jnp.stack([tick_zero, tick_one])[None]

    own_flags = trade_flags[own_rank % half_span] == 1
    mask_five = own_flags[None, :, None, None, None]
    mask_four = own_flags[None, :, None, None]
    gate_up_moved = jnp.where(mask_five, traded[0], gate_up)
    down_moved = jnp.where(mask_four, traded[1], down_proj)
    first_moved = jnp.where(mask_four, traded[2], first_moment)
    second_moved = jnp.where(mask_four, traded[3], second_moment)
    return (layer_out, gate_up_moved, down_moved, first_moved, second_moved)


def solution(mesh):
    return jax.shard_map(
        per_device,
        mesh=mesh,
        in_specs=(
            P(None, ("expert", "dp"), None),
            P(("expert", "dp"), None),
            P("section", None),
            P("section", "expert", None, "dp", None),
            P("section", "expert", "dp", None),
            P("section", "expert", "dp", None),
            P("section", "expert", "dp", None),
            P("section", None, ("expert", "dp"), None),
            P("section", None, ("expert", "dp"), None),
            P(),
        ),
        out_specs=(
            P("section", None, ("expert", "dp"), None),
            P("section", "expert", None, "dp", None),
            P("section", "expert", "dp", None),
            P("section", "expert", "dp", None),
            P("section", "expert", "dp", None),
        ),
        check_vma=False,
    )
```

time: 781 us -> 499 us (0.64)
  waiting for transfers between devices: 633 us -> 4.91 us
  Pallas kernels: 0 us -> 381 us
  blocking collectives: 34.4 us -> 0 us
  between operations: 14.3 us -> 0.79 us
  matrix products: 62.9 us -> 76.2 us
    all_gather x4 -> x0, waiting for transfers between devices: 425 us -> none  [the longest x2 257 us: layer(): arrived = lax.all_gather(normed, 'expert', axis=0, tiled=True)]
    pallas_call x0 -> x4, Pallas kernels: none -> 381 us  [the longest x1 214 us: gather_weights(): pl.pallas_call(weights_kernel, out_shape=(jax.ShapeDtypeStruct((2, 4 * ga...]
    reduce_scatter x2 -> x0, waiting for transfers between devices: 194 us -> none  [layer(): lax.psum_scatter(result, 'expert', scatter_dimension=0, tiled=True)]
    all_gather x1 -> x0, blocking collectives: 34.4 us -> none  [per_device(): all_mix = lax.all_gather(dense_mix, 'expert', axis=1, tiled=True)]
    dot_general x6 -> x4, matrix products: 62.9 us -> 76.2 us  [the longest x2 52 us: expert_ffn(): result = jnp.dot(active, down, preferred_element_type=jnp.float32)]
    ppermute x1, waiting for transfers between devices: 13.2 us -> 4.9 us  [shifted(): return lax.ppermute(value, axis, route)]
  transfers between devices with their start and end apart: 11 -> 5, of which waited for: 7 -> 1; matrix products, arithmetic and copies ran while one was open for 6% -> 11% of each run, Pallas kernels for 0% -> 43%
where the time goes in v2:
time: 499 us; the launch traced here: 497 us
  Pallas kernels  381 us (76%)
  matrix products  76.2 us (15%)
  other arithmetic  18.7 us (4%)
  starting transfers between devices  9.18 us (2%)
  local copies, waits for them, and re-layouts  6.98 us (1%)
    pallas_call x1, Pallas kernels, gather_weights(): pl.pallas_call(weights_kernel, out_shape=(jax.ShapeDtypeStruct((2, 4 * ga...  214 us
    pallas_call x2, Pallas kernels, combine(): pl.pallas_call(combine_kernel, out_shape=jax.ShapeDtypeStruct(inputs.shap...  113 us
    pallas_call x1, Pallas kernels, gather_tokens(): pl.pallas_call(tokens_kernel, out_shape=jax.ShapeDtypeStruct((EXPERTS * t...  54.3 us
    dot_general x2, matrix products, expert_ffn(): result = jnp.dot(active, down, preferred_element_type=jnp.float32)  52 us
    dot_general x2, matrix products, expert_ffn(): up_part = jnp.dot(rows_in, gate_up[1], preferred_element_type=jnp.float32)  24.1 us
  transfers between devices with their start and end apart: 5, of which 1 were waited for; matrix products, arithmetic and copies ran while one was open for 11% of the time, Pallas kernels for 43%

profile of v2, /device:TPU:2, one launch (start us, length us, event | category | flops | bytes accessed | tf_op | source)
XLA Modules:
  0.0 497.2 jit_solution(1937942403414475229)
XLA Ops:
  0.6 4.0 collective-permute-start.2
  4.7 3.4 collective-permute-start.1
  9.6 0.8 bitcast_add_fusion
  10.6 1.5 fusion.22
  12.1 1.0 select_reduce_fusion.2.mix
  13.1 1.7 fusion.24.tokens
  14.8 213.6 %gather_weights.1 = (bf16[2,4096,768]{2,1,0:T(8,128)(2,1)}, bf16[768,4096]{1,0:T(8,128)(2,1)}, bf16[1024,4096]{1,0:T(8,128)(2,1)}, f32[1024,128]{1,0:T(8,128)}) custom-call(bf16[2,1024,768]{2,1,0:T(8,128)(2,1)} %bitcast.44, bf16[192,4096]{1,0:T(8,128)(2,1)} %bitcast.45, bf16[64,4096]{1,0:T(8,128)(2,1)} %fusion.24.tokens, f32[64,128]{1,0:T(8,128)} %select_reduce_fusion.2.mix), custom_call_target="tpu_custom_call" | custom-call | tf_op jit(solution)/shard_map/gather_weights/pallas_call | solution.py:148
  228.4 12.1 %fusion.2 = f32[1024,768]{1,0:T(8,128)} fusion(bf16[1024,4096]{1,0:T(8,128)(2,1)} %get-tuple-element.14, bf16[2,4096,768]{2,1,0:T(8,128)(2,1)} %get-tuple-element.15), kind=kOutput, calls=%fused_computation.4 | convolution fusion | flops 6442450944 | bytes 17825792 | tf_op jit(solution)/shard_map/dot_general | solution.py:271
  240.8 26.0 %multiply_convert_fusion.1.partial = bf16[1024,4096]{1,0:T(8,128)(2,1)} fusion(f32[1024]{0:T(1024)S(1)} %get-tuple-element.23, bf16[768,4096]{1,0:T(8,128)(2,1)} %get-tuple-element.16, f32[1024,768]{1,0:T(8,128)} %fusion.2, bf16[1024,4096]{1,0:T(8,128)(2,1)} %get-tuple-element.14, bf16[2,4096,768]{2,1,0:T(8,128)(2,1)} %get-tuple-element.15), kind=kOutput, calls=%fused_computation.1 | convolution fusion | flops 12898009088 | bytes 32509952 | tf_op jit(solution)/shard_map/dot_general | solution.py:273
  267.4 3.4 copy-done
  270.8 55.9 %combine.2 = bf16[64,4096]{1,0:T(8,128)(2,1)S(1)} custom-call(bf16[1024,4096]{1,0:T(8,128)(2,1)S(1)} %copy-done, bf16[64,4096]{1,0:T(8,128)(2,1)S(1)} %get-tuple-element.28.inputs), custom_call_target="tpu_custom_call" | custom-call | tf_op jit(solution)/shard_map/combine/pallas_call | solution.py:237
  326.7 1.6 collective-permute-start.4
  328.3 2.0 broadcast_select_fusion.3
  330.3 2.1 broadcast_select_fusion.2
  332.4 2.2 broadcast_select_fusion.1
  334.5 2.8 broadcast_select_fusion
  337.4 4.9 collective-permute-done.4
  342.6 1.0 fusion.27.tokens
  343.6 54.3 %gather_tokens.1 = bf16[1024,4096]{1,0:T(8,128)(2,1)} custom-call(bf16[64,4096]{1,0:T(8,128)(2,1)} %fusion.27.tokens), custom_call_target="tpu_custom_call" | custom-call | tf_op jit(solution)/shard_map/gather_tokens/pallas_call | solution.py:174
  397.8 12.1 %fusion = f32[1024,768]{1,0:T(8,128)} fusion(bf16[1024,4096]{1,0:T(8,128)(2,1)} %gather_tokens.1, bf16[2,4096,768]{2,1,0:T(8,128)(2,1)} %get-tuple-element.15), kind=kOutput, calls=%fused_computation.2 | convolution fusion | flops 6442450944 | bytes 17825792 | tf_op jit(solution)/shard_map/dot_general | solution.py:271
  409.9 26.0 %multiply_convert_fusion.partial = bf16[1024,4096]{1,0:T(8,128)(2,1)} fusion(f32[1024]{0:T(1024)S(1)} %get-tuple-element.24, bf16[768,4096]{1,0:T(8,128)(2,1)} %get-tuple-element.16, f32[1024,768]{1,0:T(8,128)} %fusion, bf16[1024,4096]{1,0:T(8,128)(2,1)} %gather_tokens.1, bf16[2,4096,768]{2,1,0:T(8,128)(2,1)} %get-tuple-element.15), kind=kOutput, calls=%fused_computation | convolution fusion | flops 12898009088 | bytes 32509952 | tf_op jit(solution)/shard_map/dot_general | solution.py:273
  435.9 3.4 copy-done.1
  439.3 56.9 %combine.3 = bf16[64,4096]{1,0:T(8,128)(2,1)S(1)} custom-call(bf16[1024,4096]{1,0:T(8,128)(2,1)S(1)} %copy-done.1, bf16[64,4096]{1,0:T(8,128)(2,1)S(1)} %get-tuple-element.26.inputs), custom_call_target="tpu_custom_call" | custom-call | tf_op jit(solution)/shard_map/combine/pallas_call | solution.py:237
  496.2 1.1 maximum_bitcast_fusion
  (35 shorter events, 3.1 us)
Async XLA Ops:
  0.6 266.8 %collective-permute-start.2 = (bf16[1,1,192,4096]{3,2,1,0:T(8,128)(2,1)}, bf16[1,1,192,4096]{3,2,1,0:T(8,128)(2,1)S(1)}, u32[]{:S(2)}, u32[]{:S(2)}) collective-permute-start(bf16[1,1,192,4096]{3,2,1,0:T(8,128)(2,1)} %param.15), channel_id=1, source_target_pairs={{0,32},{4,36},{8,40},{12,44},{16,48},{20,52},{24,56},{28,60},{32,0... | collective-permute-start | bytes 4718600 | tf_op jit(solution)/shard_map/ppermute | solution.py:254
  4.6 262.8 %collective-permute-start.3 = (bf16[1,1,192,4096]{3,2,1,0:T(8,128)(2,1)}, bf16[1,1,192,4096]{3,2,1,0:T(8,128)(2,1)}, u32[]{:S(2)}, u32[]{:S(2)}) collective-permute-start(bf16[1,1,192,4096]{3,2,1,0:T(8,128)(2,1)} %param.16), channel_id=1, source_target_pairs={{0,32},{4,36},{8,40},{12,44},{16,48},{20,52},{24,56},{28,60},{32,0... | collective-permute-start | bytes 4718600 | tf_op jit(solution)/shard_map/ppermute | solution.py:254
  4.7 262.7 %collective-permute-start.1 = (bf16[1,1,192,4096]{3,2,1,0:T(8,128)(2,1)}, bf16[1,1,192,4096]{3,2,1,0:T(8,128)(2,1)}, u32[]{:S(2)}, u32[]{:S(2)}) collective-permute-start(bf16[1,1,192,4096]{3,2,1,0:T(8,128)(2,1)} %param.14), channel_id=1, source_target_pairs={{0,32},{4,36},{8,40},{12,44},{16,48},{20,52},{24,56},{28,60},{32,0... | collective-permute-start | bytes 4718600 | tf_op jit(solution)/shard_map/ppermute | solution.py:254
  8.1 259.3 %collective-permute-start = (bf16[1,1,2,1024,768]{4,3,2,1,0:T(8,128)(2,1)}, bf16[1,1,2,1024,768]{4,3,2,1,0:T(8,128)(2,1)}, u32[]{:S(2)}, u32[]{:S(2)}) collective-permute-start(bf16[1,1,2,1024,768]{4,3,2,1,0:T(8,128)(2,1)} %param.13), channel_id=1, source_target_pairs={{0,32},{4,36},{8,40},{12,44},{16,48},{20,52},{24,56},{28,60},{32,0... | collective-permute-start | bytes 9437192 | tf_op jit(solution)/shard_map/ppermute | solution.py:254
  228.3 12.1 %copy-start.7 = (f32[1024,128]{1,0:T(8,128)S(1)}, f32[1024,128]{1,0:T(8,128)}, u32[]{:S(2)}) copy-start(f32[1024,128]{1,0:T(8,128)} %get-tuple-element.17) | copy-start | bytes 1572868
  240.8 26.0 %copy-start.9 = (s32[8,1]{0,1:T(1,128)S(1)}, s32[8,1]{0,1:T(1,128)}, u32[]{:S(2)}) copy-start(s32[8,1]{0,1:T(1,128)} %param.19) | copy-start | bytes 100
  267.4 3.4 copy-start
  270.8 57.5 %copy-start.3 = (bf16[1,1,192,4096]{3,2,1,0:T(8,128)(2,1)S(1)}, bf16[1,1,192,4096]{3,2,1,0:T(8,128)(2,1)}, u32[]{:S(2)}) copy-start(bf16[1,1,192,4096]{3,2,1,0:T(8,128)(2,1)} %param.14) | copy-start | bytes 4718596
  326.7 3.6 copy-start.4
  326.7 15.6 %collective-permute-start.4 = (bf16[64,4096]{1,0:T(8,128)(2,1)S(1)}, bf16[64,4096]{1,0:T(8,128)(2,1)S(1)}, u32[]{:S(2)}, u32[]{:S(2)}) collective-permute-start(bf16[64,4096]{1,0:T(8,128)(2,1)S(1)} %combine.2), channel_id=1, source_target_pairs={{0,64},{1,65},{2,66},{3,67},{4,68},{5,69},{6,70},{7,71},{8,72},{9,... | collective-permute-start | bytes 1572872 | tf_op jit(solution)/shard_map/ppermute | solution.py:260
  330.3 2.1 copy-start.5
  332.4 2.2 copy-start.2
  334.5 7.7 %copy-start.6 = (bf16[2,64,4096]{2,1,0:T(8,128)(2,1)S(1)}, bf16[2,64,4096]{2,1,0:T(8,128)(2,1)}, u32[]{:S(2)}) copy-start(bf16[2,64,4096]{2,1,0:T(8,128)(2,1)} %param.10) | copy-start | bytes 3145732
  334.5 8.0 %copy-start.8 = (f32[1,4096]{1,0:T(1,128)S(1)}, f32[1,4096]{1,0:T(1,128)}, u32[]{:S(2)}) copy-start(f32[1,4096]{1,0:T(1,128)} %param.12) | copy-start | bytes 49156
  435.9 3.4 copy-start.1

commit v3 on v1

v3 whole, which is shorter than its diff:
```python
import functools

import jax
import jax.numpy as jnp
from jax import lax
from jax.experimental import pallas as pl
from jax.experimental.pallas import tpu as pltpu
from jax.sharding import PartitionSpec as P

EXPERTS = 16
BLOCK = 64
PLANE = 4 * BLOCK
TILE = 256
MESH = pl.DeviceIdType.MESH
ANY = pl.BlockSpec(memory_space=pl.ANY)
VMEM = pl.BlockSpec(memory_space=pltpu.VMEM)
DMA = pltpu.SemaphoreType.DMA
STEPS = (1, 3, 2)
HOMES = (0, 3, 1, 2)


def along_z(rank, step):
    return lax.rem(rank + 4 * step, EXPERTS)


def remote(src, dst, sems, device):
    return pltpu.make_async_remote_copy(
        src_ref=src,
        dst_ref=dst,
        send_sem=sems[0],
        recv_sem=sems[1],
        device_id=device,
        device_id_type=MESH,
    )


def greet(devices):
    barrier = pltpu.get_barrier_semaphore()
    for device in devices:
        pl.semaphore_signal(barrier, inc=1, device_id=device, device_id_type=MESH)
    pl.semaphore_wait(barrier, len(devices))


def group(rank):
    return [{"expert": along_z(rank, step)} for step in STEPS] + [
        {"expert": rank ^ 2},
        {"expert": rank ^ 1},
    ]


def over_tiles(low, high, body):
    @pl.loop(0, BLOCK // 16)
    def _(r):
        rows = pl.ds(pl.multiple_of(r * 16, 16), 16)

        @pl.loop(low // 512, high // 512)
        def _(c):
            body(rows, pl.ds(pl.multiple_of(c * 512, 512), 512))


class Spread:
    def __init__(self, whole, cut, sems, rank):
        self.whole, self.cut, self.rank = whole, cut, rank
        self.width = whole.shape[1]
        self.sems = sems
        self.sources = [along_z(rank, 4 - step) for step in STEPS]
        self.sent = []
        own = self.at(rank)
        self.first = [
            self.copy(own, i, {"expert": along_z(rank, step)}) for i, step in enumerate(STEPS)
        ]
        self.first.append(self.copy(own, 3, {"expert": rank ^ 2}))
        self.first.append(self.copy(own, 4, {"expert": rank ^ 1}))
        self.over_x, self.over_z, self.siblings = [], [], {}

    def at(self, owner, low=0, high=None):
        rows = pl.ds(pl.multiple_of(owner * BLOCK, BLOCK), BLOCK)
        if low == 0 and high is None:
            return self.whole.at[rows]
        return self.whole.at[rows, pl.ds(low, high - low)]

    def copy(self, ref, i, device):
        return remote(ref, ref, (self.sems[0].at[i], self.sems[1].at[i]), device)

    def start(self, copy):
        copy.start()
        self.sent.append(copy)
        return copy

    def begin(self):
        for copy in self.first:
            self.start(copy)

    def to_sibling(self, key, owner, i):
        self.siblings[key] = self.start(self.copy(self.at(owner), i, {"expert": self.rank ^ 1}))

    def forward_x_arrival(self):
        self.first[3].wait_recv()
        if self.cut < self.width:
            for i, step in enumerate(STEPS):
                ref = self.at(self.rank ^ 2, self.cut, self.width)
                self.over_z.append(
                    self.start(self.copy(ref, 8 + i, {"expert": along_z(self.rank, step)}))
                )
        self.to_sibling("x", self.rank ^ 2, 11)

    def forward_z_arrival(self, i):
        self.first[i].wait_recv()
        high = None if self.cut == self.width else self.cut
        self.over_x.append(
            self.start(self.copy(self.at(self.sources[i], 0, high), 5 + i, {"expert": self.rank ^ 2}))
        )
        self.to_sibling(("z", i), self.sources[i], 12 + i)

    def forward_far_arrival(self, i):
        self.over_x[i].wait_recv()
        if self.over_z:
            self.over_z[i].wait_recv()
        self.to_sibling(("far", i), self.sources[i] ^ 2, 15 + i)

    def wait_own_plane(self):
        self.first[4].wait_recv()
        self.siblings["x"].wait_recv()

    def wait_plane(self, i):
        self.siblings[("z", i)].wait_recv()
        self.siblings[("far", i)].wait_recv()

    def finish(self):
        for copy in self.sent:
            copy.wait_send()


class Combine:
    def __init__(self, partial, theirs, over_x, from_z, halves, last, cut, sems, rank):
        self.partial, self.theirs, self.over_x, self.from_z = partial, theirs, over_x, from_z
        self.halves, self.last, self.cut, self.rank = halves, last, cut, rank
        self.width = partial.shape[2]
        self.send, self.recv = sems
        self.side = lax.rem(rank // 2, 2)
        self.core = lax.rem(rank, 2)
        self.sent = []
        self.sibling, self.x_copies, self.z_copies, self.half_copies = {}, {}, {}, {}

    def start(self, src, dst, i, device):
        copy = remote(src, dst, (self.send.at[i], self.recv.at[i]), {"expert": device})
        copy.start()
        self.sent.append(copy)
        return copy

    def rows(self, dx, core):
        side = self.side if dx == 0 else 1 - self.side
        return pl.multiple_of((side * 2 + core) * BLOCK, BLOCK)

    def to_sibling(self, m):
        for dx in (1, 0):
            src = self.partial.at[m, pl.ds(self.rows(dx, 1 - self.core), BLOCK)]
            self.sibling[m, dx] = self.start(src, self.theirs.at[m, dx], 2 * m + dx, self.rank ^ 1)

    def add_sibling(self, m):
        peer = along_z(self.rank, HOMES[m])
        for dx in (1, 0):
            self.sibling[m, dx].wait_recv()
            base = self.rows(dx, self.core)

            def body(rows, columns):
                mine = self.partial[m, pl.ds(pl.multiple_of(base + rows.start, 16), 16), columns]
                total = mine.astype(jnp.float32) + self.theirs[m, dx, rows, columns].astype(jnp.float32)
                self.theirs[m, dx, rows, columns] = total.astype(jnp.bfloat16)

            over_tiles(0, self.width, body)
            if dx == 1:
                below = pl.ds(0, self.cut)
                self.x_copies[m] = self.start(
                    self.theirs.at[m, 1, :, below], self.over_x.at[m, :, below], 8 + m, self.rank ^ 2
                )
            if self.cut < self.width and m:
                above = pl.ds(self.cut, self.width - self.cut)
                self.half_copies[m, dx] = self.start(
                    self.theirs.at[m, dx, :, above], self.halves.at[m - 1, dx], 12 + 2 * m + dx, peer
                )

    def add_x(self, m):
        self.x_copies[m].wait_recv()

        def body(rows, columns):
            total = self.over_x[m, rows, columns].astype(jnp.float32)
            total = total + self.theirs[m, 0, rows, columns].astype(jnp.float32)
            self.over_x[m, rows, columns] = total.astype(jnp.bfloat16)

        over_tiles(0, self.cut, body)
        if m:
            below = pl.ds(0, self.cut)
            self.z_copies[m] = self.start(
                self.over_x.at[m, :, below], self.from_z.at[m - 1, :, below], 20 + m,
                along_z(self.rank, HOMES[m]),
            )

    def finish(self, inputs, out):
        cut, width = self.cut, self.width
        if cut < width:
            for m in (1, 2, 3):
                for dx in (1, 0):
                    self.half_copies[m, dx].wait_recv()

            def gathered(dx, rows, columns):
                total = self.theirs[0, dx, rows, columns].astype(jnp.float32)
                inner = pl.ds(pl.multiple_of(columns.start - cut, 512), 512)
                for m in range(3):
                    total = total + self.halves[m, dx, rows, inner].astype(jnp.float32)
                return total

            def other(rows, columns):
                self.theirs[0, 1, rows, columns] = gathered(1, rows, columns).astype(jnp.bfloat16)

            over_tiles(cut, width, other)
            above = pl.ds(cut, width - cut)
            copy = self.start(self.theirs.at[0, 1, :, above], self.last, 24, self.rank ^ 2)

        for m in (1, 2, 3):
            self.z_copies[m].wait_recv()

        def near(rows, columns):
            total = inputs[rows, columns].astype(jnp.float32)
            total = total + self.over_x[0, rows, columns].astype(jnp.float32)
            for m in range(3):
                total = total + self.from_z[m, rows, columns].astype(jnp.float32)
            out[rows, columns] = total.astype(jnp.bfloat16)

        over_tiles(0, cut, near)
        if cut < width:
            copy.wait_recv()

            def far(rows, columns):
                inner = pl.ds(pl.multiple_of(columns.start - cut, 512), 512)
                total = inputs[rows, columns].astype(jnp.float32) + gathered(0, rows, columns)
                total = total + self.last[rows, inner].astype(jnp.float32)
                out[rows, columns] = total.astype(jnp.bfloat16)

            over_tiles(cut, width, far)
        for sent in self.sent:
            sent.wait_send()


def norm_into(inputs, gain, whole, rank):
    @pl.loop(0, BLOCK // 16)
    def _(r):
        values = inputs[pl.ds(pl.multiple_of(r * 16, 16), 16), :].astype(jnp.float32)
        mean = jnp.mean(values * values, axis=-1, keepdims=True)
        normed = (values * lax.rsqrt(mean + 1e-06) * gain[...]).astype(jnp.bfloat16)
        whole[pl.ds(pl.multiple_of(rank * BLOCK + r * 16, 16), 16), :] = normed


def hidden(tokens, gate_up, active, first_row, active_row):
    @pl.loop(0, gate_up.shape[2] // TILE)
    def _(n):
        columns = pl.ds(pl.multiple_of(n * TILE, TILE), TILE)
        rows_in = tokens[pl.ds(first_row, PLANE), :]
        gate = jnp.dot(rows_in, gate_up[0, :, columns], preferred_element_type=jnp.float32)
        up = jnp.dot(rows_in, gate_up[1, :, columns], preferred_element_type=jnp.float32)
        active[pl.ds(active_row, PLANE), columns] = (jax.nn.silu(gate) * up).astype(jnp.bfloat16)


def project(active, down, all_mix, partial, m, first_row, active_row, lane):
    mix = all_mix[pl.ds(first_row, PLANE), :]
    lanes = lax.broadcasted_iota(jnp.int32, mix.shape, 1)
    weight = jnp.sum(jnp.where(lanes == lane, mix, 0.0), axis=-1, keepdims=True)

    @pl.loop(0, down.shape[1] // TILE)
    def _(n):
        columns = pl.ds(pl.multiple_of(n * TILE, TILE), TILE)
        result = jnp.dot(
            active[pl.ds(active_row, PLANE), :], down[:, columns], preferred_element_type=jnp.float32
        )
        partial[m, :, columns] = (result * weight).astype(jnp.bfloat16)


def plane_row(rank, m):
    return pl.multiple_of(along_z(rank, HOMES[m]) // 4 * PLANE, PLANE)


def first_kernel(
    inputs, gain, mix, gate_up, down, first, second,
    full_gate_up, full_down, got_gate_up, got_down, got_first, got_second, mix_out, out,
    tokens, all_mix, w_gate_up, w_down, active, partial, theirs, over_x, from_z,
    y_send, y_recv, here, trade_send, trade_recv, d_send, d_recv, m_send, m_recv, c_send, c_recv,
):
    rank, place = lax.axis_index("expert"), lax.axis_index("dp")
    right, left = lax.rem(place + 1, 4), lax.rem(place + 3, 4)
    width = inputs.shape[1]
    greet([{"dp": right}, {"dp": left}] + group(rank))
    deep, low = gate_up.shape[1], down.shape[0]
    half = low // 2

    def gate_part(ref, k, owner):
        return ref.at[k, pl.ds(pl.multiple_of(owner * deep, deep), deep)]

    def down_part(ref, k, owner):
        return ref.at[pl.ds(pl.multiple_of(owner * low + k * half, half), half)]

    own = [gate_up.at[0], gate_up.at[1], down.at[pl.ds(0, half)], down.at[pl.ds(half, half)]]
    parts = [functools.partial(gate_part, full_gate_up, 0), functools.partial(gate_part, full_gate_up, 1),
             functools.partial(down_part, full_down, 0), functools.partial(down_part, full_down, 1)]
    nearby = [functools.partial(gate_part, w_gate_up, 0), functools.partial(gate_part, w_gate_up, 1),
              functools.partial(down_part, w_down, 0), functools.partial(down_part, w_down, 1)]

    def sems(k, i):
        return (y_send.at[k, i], y_recv.at[k, i])

    ways = [
        (remote(own[k], parts[k](place), sems(k, 0), {"dp": right}),
         remote(own[k], parts[k](place), sems(k, 1), {"dp": left}))
        for k in range(4)
    ]
    passes = [
        remote(parts[k](left), parts[k](left), sems(k, 2), {"dp": right}) if k % 2 == 0
        else remote(parts[k](right), parts[k](right), sems(k, 2), {"dp": left})
        for k in range(4)
    ]
    local = []

    def local_copy(src, dst, i):
        copy = pltpu.make_async_copy(src, dst, here.at[i])
        copy.start()
        local.append(copy)
        return copy

    def send_own(k):
        ways[k][0].start()
        ways[k + 1][1].start()
        ways[k + 1][0].start()
        ways[k][1].start()

    opposite = lax.rem(place + 2, 4)
    send_own(0)
    norm_into(inputs, gain, tokens, rank)
    spread = Spread(tokens, width, (d_send, d_recv), rank)
    spread.begin()
    all_mix[pl.ds(pl.multiple_of(rank * BLOCK, BLOCK), BLOCK), :] = mix[...]
    mixes = Spread(all_mix, all_mix.shape[1], (m_send, m_recv), rank)
    mixes.begin()
    for k in range(4):
        local_copy(own[k], parts[k](place), k)
        local_copy(own[k], nearby[k](place), 4 + k)

    spreads = (spread, mixes)
    for one in spreads:
        one.forward_x_arrival()
    for i in range(3):
        for one in spreads:
            one.forward_z_arrival(i)
    trades = []
    for i, (src, dst) in enumerate(
        ((gate_up, got_gate_up), (down, got_down), (first, got_first), (second, got_second))
    ):
        copy = remote(src, dst, (trade_send.at[i], trade_recv.at[i]), {"expert": rank ^ 8})
        copy.start()
        trades.append(copy)

    def pass_on(k):
        for j in (k, k + 1):
            ways[j][j % 2].wait_recv()
            passes[j].start()

    def land(k):
        for j in (k, k + 1):
            ways[j][1 - j % 2].wait_recv()
            local_copy(parts[j](left), nearby[j](left), 8 + j)
            local_copy(parts[j](right), nearby[j](right), 12 + j)

    def land_passed(k):
        for j in (k, k + 1):
            passes[j].wait_recv()
            local_copy(parts[j](opposite), nearby[j](opposite), 16 + j)

    pass_on(0)
    send_own(2)
    land(0)
    for i in range(3):
        for one in spreads:
            one.forward_far_arrival(i)
    for one in spreads:
        one.wait_own_plane()
        for i in range(3):
            one.wait_plane(i)
    land_passed(0)
    pass_on(2)
    land(2)
    for copy in local:
        copy.wait()
    local.clear()

    @pl.loop(0, 4)
    def _(b):
        row = pl.multiple_of(b * PLANE, PLANE)
        hidden(tokens, w_gate_up, active, row, row)

    land_passed(2)
    for copy in local:
        copy.wait()
    local.clear()
    keep = local_copy(all_mix, mix_out, 0)

    combine = Combine(partial, theirs, over_x, from_z, None, None, width, (c_send, c_recv), rank)
    order = (3, 1, 2, 0)
    for i, m in enumerate(order):
        row = plane_row(rank, m)
        project(active, w_down, all_mix, partial, m, row, row, rank)
        combine.to_sibling(m)
        if i:
            combine.add_sibling(order[i - 1])
        if i > 1:
            combine.add_x(order[i - 2])
    combine.add_sibling(order[3])
    combine.add_x(order[2])
    combine.add_x(order[3])
    combine.finish(inputs, out)
    keep.wait()
    for one in spreads:
        one.finish()
    for k in range(4):
        ways[k][0].wait_send()
        ways[k][1].wait_send()
        passes[k].wait_send()
    for copy in trades:
        copy.wait_recv()
    for copy in trades:
        copy.wait_send()


def bf16(*shape):
    return jax.ShapeDtypeStruct(shape, jnp.bfloat16)


def token_scratch(width, hidden_width, active_rows):
    return [
        pltpu.VMEM((2, width, hidden_width), jnp.bfloat16),
        pltpu.VMEM((hidden_width, width), jnp.bfloat16),
        pltpu.VMEM((active_rows, hidden_width), jnp.bfloat16),
        pltpu.VMEM((4, PLANE, width), jnp.bfloat16),
        pltpu.VMEM((4, 2, BLOCK, width), jnp.bfloat16),
        pltpu.VMEM((4, BLOCK, width), jnp.bfloat16),
        pltpu.VMEM((3, BLOCK, width), jnp.bfloat16),
    ]


def first_tick(inputs, gain, mix, gate_up, down, first, second):
    width, hidden_width = inputs.shape[1], gate_up.shape[2]
    rows = EXPERTS * BLOCK
    return pl.pallas_call(
        first_kernel,
        out_shape=(
            bf16(2, width, hidden_width), bf16(hidden_width, width),
            bf16(*gate_up.shape), bf16(*down.shape), bf16(*down.shape), bf16(*down.shape),
            jax.ShapeDtypeStruct((rows, 128), jnp.float32), bf16(*inputs.shape),
        ),
        in_specs=[VMEM] * 3 + [ANY] * 4,
        out_specs=[ANY] * 7 + [VMEM],
        scratch_shapes=[
            pltpu.VMEM((rows, width), jnp.bfloat16),
            pltpu.VMEM((rows, 128), jnp.float32),
            *token_scratch(width, hidden_width, rows),
            DMA((4, 3)), DMA((4, 3)), DMA((20,)), DMA((4,)), DMA((4,)),
            DMA((18,)), DMA((18,)), DMA((18,)), DMA((18,)), DMA((25,)), DMA((25,)),
        ],
        compiler_params=pltpu.CompilerParams(
            collective_id=0, has_side_effects=True, vmem_limit_bytes=60 << 20
        ),
        name="first_tick",
    )(inputs, gain, mix, gate_up, down, first, second)


def second_kernel(
    cut, inputs, gain, mix, full_gate_up, full_down, out,
    tokens, w_gate_up, w_down, active, partial, theirs, over_x, from_z, halves, last,
    here, d_send, d_recv, c_send, c_recv,
):
    rank = lax.axis_index("expert")
    greet(group(rank))
    loads = []
    for i, (src, dst) in enumerate(((full_gate_up, w_gate_up), (full_down, w_down))):
        copy = pltpu.make_async_copy(src, dst, here.at[i])
        copy.start()
        loads.append(copy)
    norm_into(inputs, gain, tokens, rank)
    spread = Spread(tokens, cut, (d_send, d_recv), rank)
    spread.begin()
    combine = Combine(partial, theirs, over_x, from_z, halves, last, cut, (c_send, c_recv), rank)

    def compute(m):
        row = plane_row(rank, m)
        hidden(tokens, w_gate_up, active, row, 0)
        project(active, w_down, mix, partial, m, row, 0, EXPERTS + rank)
        combine.to_sibling(m)

    spread.forward_x_arrival()
    for i in range(3):
        spread.forward_z_arrival(i)
    for copy in loads:
        copy.wait()
    spread.wait_own_plane()
    compute(0)
    spread.forward_far_arrival(0)
    spread.forward_far_arrival(1)
    combine.add_sibling(0)
    spread.wait_plane(0)
    compute(1)
    spread.forward_far_arrival(2)
    combine.add_x(0)
    combine.add_sibling(1)
    spread.wait_plane(1)
    compute(2)
    combine.add_x(1)
    combine.add_sibling(2)
    spread.wait_plane(2)
    compute(3)
    combine.add_x(2)
    combine.add_sibling(3)
    combine.add_x(3)
    combine.finish(inputs, out)
    spread.finish()


def second_tick(inputs, gain, mix, full_gate_up, full_down):
    width, hidden_width = inputs.shape[1], full_gate_up.shape[2]
    cut = 2560
    return pl.pallas_call(
        functools.partial(second_kernel, cut),
        out_shape=bf16(*inputs.shape),
        in_specs=[VMEM] * 3 + [ANY] * 2,
        out_specs=VMEM,
        scratch_shapes=[
            pltpu.VMEM((EXPERTS * BLOCK, width), jnp.bfloat16),
            *token_scratch(width, hidden_width, PLANE),
            pltpu.VMEM((3, 2, BLOCK, width - cut), jnp.bfloat16),
            pltpu.VMEM((BLOCK, width - cut), jnp.bfloat16),
            DMA((2,)), DMA((18,)), DMA((18,)), DMA((25,)), DMA((25,)),
        ],
        compiler_params=pltpu.CompilerParams(
            collective_id=1, has_side_effects=True, vmem_limit_bytes=60 << 20
        ),
        name="second_tick",
    )(inputs, gain, mix, full_gate_up, full_down)


def shifted(value, axis, distance):
    devices = range(lax.axis_size(axis))
    route = [(i - distance, i) for i in devices if i - distance in devices]
    return lax.ppermute(value, axis, route)


def per_device(
    fresh_tokens,
    in_flight,
    norm_weight,
    gate_up,
    down_proj,
    first_moment,
    second_moment,
    route_ids,
    route_probs,
    trade_flags,
):
    half_span = lax.axis_size("expert") // 2
    own_rank = lax.axis_index("expert")
    section_index = lax.axis_index("section")

    lanes = jnp.arange(128, dtype=jnp.int32)
    probs = route_probs[0]
    mix = probs / jnp.sum(probs, axis=-1, keepdims=True)
    wanted = route_ids[0] + EXPERTS * jnp.arange(2, dtype=jnp.int32)[:, None, None]
    dense_mix = jnp.sum(jnp.where(wanted[..., None] == lanes, mix[..., None], 0.0), axis=(0, 2))

    first_input = jnp.where(section_index == 0, fresh_tokens[0], in_flight)
    full_gate_up, full_down, *traded, all_mix, tick_zero = first_tick(
        first_input, norm_weight, dense_mix,
        gate_up[0, 0], down_proj[0, 0], first_moment[0, 0], second_moment[0, 0],
    )
    arrived = shifted(tick_zero, "section", 1)
    second_input = jnp.where(section_index == 0, fresh_tokens[1], arrived)
    tick_one = second_tick(second_input, norm_weight, all_mix, full_gate_up, full_down)
    layer_out = jnp.stack([tick_zero, tick_one])[None]

    moves = trade_flags[own_rank % half_span, 0] == 1
    kept = (gate_up, down_proj, first_moment, second_moment)
    moved = [
        jnp.where(moves, got.reshape(own.shape), own) for got, own in zip(traded, kept)
    ]
    return (layer_out, *moved)


def solution(mesh):
    return jax.shard_map(
        per_device,
        mesh=mesh,
        in_specs=(
            P(None, ("expert", "dp"), None),
            P(("expert", "dp"), None),
            P("section", None),
            P("section", "expert", None, "dp", None),
            P("section", "expert", "dp", None),
            P("section", "expert", "dp", None),
            P("section", "expert", "dp", None),
            P("section", None, ("expert", "dp"), None),
            P("section", None, ("expert", "dp"), None),
            P(),
        ),
        out_specs=(
            P("section", None, ("expert", "dp"), None),
            P("section", "expert", None, "dp", None),
            P("section", "expert", "dp", None),
            P("section", "expert", "dp", None),
            P("section", "expert", "dp", None),
        ),
        check_vma=False,
    )
```

time: 781 us -> 355 us (0.45)
  waiting for transfers between devices: 633 us -> 1.38 us
  Pallas kernels: 0 us -> 331 us
  matrix products: 62.9 us -> 0 us
  blocking collectives: 34.4 us -> 0 us
  between operations: 14.3 us -> 0.75 us
  starting transfers between devices: 9.3 us -> 1.29 us
    all_gather x4 -> x0, waiting for transfers between devices: 425 us -> none  [the longest x2 257 us: layer(): arrived = lax.all_gather(normed, 'expert', axis=0, tiled=True)]
    pallas_call x0 -> x2, Pallas kernels: none -> 331 us  [the longest x1 230 us: first_tick(): pl.pallas_call(first_kernel, out_shape=(bf16(2, width, hidden_width), bf1...]
    reduce_scatter x2 -> x0, waiting for transfers between devices: 194 us -> none  [layer(): lax.psum_scatter(result, 'expert', scatter_dimension=0, tiled=True)]
    dot_general x6 -> x0, matrix products: 62.9 us -> none  [the longest x2 23 us: layer(): result = jnp.dot(active, down_weights, preferred_element_type=jnp.float32)]
    all_gather x1 -> x0, blocking collectives: 34.4 us -> none  [per_device(): all_mix = lax.all_gather(dense_mix, 'expert', axis=1, tiled=True)]
    ppermute x5 -> x1, waiting for transfers between devices: 13.2 us -> 1.38 us  [shifted(): return lax.ppermute(value, axis, route)]
  transfers between devices with their start and end apart: 11 -> 1, of which waited for: 7 -> 1; matrix products, arithmetic and copies ran while one was open for 6% -> 3% of each run, Pallas kernels for 0% -> 0%
where the time goes in v3:
time: 355 us; the launch traced here: 354 us
  Pallas kernels  331 us (93%)
  other arithmetic  19.7 us (6%)
    pallas_call x1, Pallas kernels, first_tick(): pl.pallas_call(first_kernel, out_shape=(bf16(2, width, hidden_width), bf1...  230 us
    pallas_call x1, Pallas kernels, second_tick(): pl.pallas_call(functools.partial(second_kernel, cut), out_shape=bf16(*inp...  101 us
    select_n x3, other arithmetic, per_device(): jnp.where(moves, got.reshape(own.shape), own)  9.87 us
  transfers between devices with their start and end apart: 1, of which 1 were waited for; matrix products, arithmetic and copies ran while one was open for 3% of the time, Pallas kernels for 0%

profile of v3, /device:TPU:2, one launch (start us, length us, event | category | flops | bytes accessed | tf_op | source)
XLA Modules:
  0.0 354.0 jit_solution(10015718338530447625)
XLA Ops:
  0.6 0.7 reduce_sum.18
  1.4 0.7 bitcast_divide_fusion
  2.1 0.8 bitcast_add_fusion
  2.8 0.1 copy.17
  2.9 0.1 copy.18
  3.0 1.0 select_reduce_fusion.mix
  4.0 2.0 bitcast_select_fusion.5.inputs
  6.1 229.9 %first_tick.1 = (bf16[2,4096,768]{2,1,0:T(8,128)(2,1)}, bf16[768,4096]{1,0:T(8,128)(2,1)}, bf16[2,1024,768]{2,1,0:T(8,128)(2,1)}, bf16[192,4096]{1,0:T(8,128)(2,...) custom-call(bf16[64,4096]{1,0:T(8,128)(2,1)} %bitcast_select_fusion., ...), custom_call_target="tpu_custom_call" | custom-call | tf_op jit(solution)/shard_map/first_tick/pallas_call | solution.py:450
  235.9 1.3 collective-permute-start
  237.3 0.0 copy-done.8
  237.3 0.6 fusion
  237.9 0.0 copy-done.1
  237.9 0.0 copy-done.2
  237.9 0.0 copy-start.4
  237.9 5.0 %bitcast_select_fusion.1 = (bf16[1,1,192,4096]{3,2,1,0:T(8,128)(2,1)}, bf16[1,1,192,4096]{3,2,1,0:T(8,128)(2,1)}) fusion(bf16[1,1,192,4096]{3,2,1,0:T(8,128)(2,1)S(1)} %copy-done.2, bf16[192,4096]{1,0:T(8,128)(2,1)} %get-tuple-element.20, pred[]{:T(512)} %bitcast.11, bf16[1,1,192,4096]{3,2,1,0:T(8,128)(2,1)S(1)} %copy-done.1, ...), kind=kLoop, calls=%fused_computation.1 | loop fusion | flops 1572864 | bytes 9437185 | tf_op jit(solution)/shard_map/jit(_where)/select_n | solution.py:587
  242.9 0.0 copy-done.3
  242.9 0.0 copy-done.5
  242.9 2.1 bitcast_select_fusion.3
  245.0 0.0 copy-done.4
  245.1 2.7 bitcast_select_fusion
  247.8 1.4 collective-permute-done
  249.2 1.9 bitcast_select_fusion.4.inputs
  251.1 100.8 %second_tick.1 = bf16[64,4096]{1,0:T(8,128)(2,1)} custom-call(bf16[64,4096]{1,0:T(8,128)(2,1)} %bitcast_select_fusion.4.inputs, f32[1,4096]{1,0:T(1,128)} %gain.3, f32[1024,128]{1,0:T(8,128)} %get-tuple-element.14.mix, bf16[2,4096,768]{2,1,0:T(8,128)(2,1)} %get-tuple-element.15.full_gate_up, bf16[768,4096]{1,0:T(8,128)(2,1)} %get-tuple-element.16.full_down), custom_call_target="tpu_custom_call" | custom-call | tf_op jit(solution)/shard_map/second_tick/pallas_call | solution.py:527
  351.9 2.1 maximum_bitcast_fusion
  (12 shorter events, 0.0 us)
Async XLA Ops:
  6.1 231.2 %copy-start.8 = (s32[8,1]{0,1:T(1,128)S(1)}, s32[8,1]{0,1:T(1,128)}, u32[]{:S(2)}) copy-start(s32[8,1]{0,1:T(1,128)} %param.19) | copy-start | bytes 100
  6.1 231.8 %copy-start.1 = (bf16[1,1,192,4096]{3,2,1,0:T(8,128)(2,1)S(1)}, bf16[1,1,192,4096]{3,2,1,0:T(8,128)(2,1)}, u32[]{:S(2)}) copy-start(bf16[1,1,192,4096]{3,2,1,0:T(8,128)(2,1)} %param.15) | copy-start | bytes 4718596
  6.1 231.8 %copy-start.2 = (bf16[1,1,192,4096]{3,2,1,0:T(8,128)(2,1)S(1)}, bf16[1,1,192,4096]{3,2,1,0:T(8,128)(2,1)}, u32[]{:S(2)}) copy-start(bf16[1,1,192,4096]{3,2,1,0:T(8,128)(2,1)} %param.16) | copy-start | bytes 4718596
  235.9 13.2 %collective-permute-start = (bf16[64,4096]{1,0:T(8,128)(2,1)}, bf16[64,4096]{1,0:T(8,128)(2,1)}, u32[]{:S(2)}, u32[]{:S(2)}) collective-permute-start(bf16[64,4096]{1,0:T(8,128)(2,1)} %get-tuple-element.13), channel_id=1, source_target_pairs={{0,64},{1,65},{2,66},{3,67},{4,68},{5,69},{6,70},{7,71},{8,72},{9,... | collective-permute-start | bytes 1572872 | tf_op jit(solution)/shard_map/ppermute | solution.py:549
  237.9 5.1 %copy-start.3 = (bf16[1,1,192,4096]{3,2,1,0:T(8,128)(2,1)S(1)}, bf16[1,1,192,4096]{3,2,1,0:T(8,128)(2,1)}, u32[]{:S(2)}) copy-start(bf16[1,1,192,4096]{3,2,1,0:T(8,128)(2,1)} %param.14) | copy-start | bytes 4718596
  237.9 5.1 %copy-start.5 = (bf16[192,4096]{1,0:T(8,128)(2,1)S(1)}, bf16[192,4096]{1,0:T(8,128)(2,1)}, u32[]{:S(2)}) copy-start(bf16[192,4096]{1,0:T(8,128)(2,1)} %get-tuple-element.18) | copy-start | bytes 4718596
  237.9 7.2 %copy-start.4 = (bf16[2,1024,768]{2,1,0:T(8,128)(2,1)S(1)}, bf16[2,1024,768]{2,1,0:T(8,128)(2,1)}, u32[]{:S(2)}) copy-start(bf16[2,1024,768]{2,1,0:T(8,128)(2,1)} %get-tuple-element.17) | copy-start | bytes 9437188
  242.9 2.1 copy-start
  245.0 4.1 %copy-start.6 = (bf16[2,64,4096]{2,1,0:T(8,128)(2,1)S(1)}, bf16[2,64,4096]{2,1,0:T(8,128)(2,1)}, u32[]{:S(2)}) copy-start(bf16[2,64,4096]{2,1,0:T(8,128)(2,1)} %param.10) | copy-start | bytes 3145732
  251.1 100.8 %copy-start.7 = (bf16[64,4096]{1,0:T(8,128)(2,1)S(1)}, bf16[64,4096]{1,0:T(8,128)(2,1)}, u32[]{:S(2)}) copy-start(bf16[64,4096]{1,0:T(8,128)(2,1)} %get-tuple-element.13) | copy-start | bytes 1572868

commit v4 on v3

--- a/solution.py
+++ b/solution.py
@@ -10,6 +10,7 @@
 EXPERTS = 16
 BLOCK = 64
 PLANE = 4 * BLOCK
+HALF = BLOCK // 2
 TILE = 256
 MESH = pl.DeviceIdType.MESH
 ANY = pl.BlockSpec(memory_space=pl.ANY)
@@ -59,8 +60,9 @@
 
 
 class Spread:
-    def __init__(self, whole, cut, sems, rank):
+    def __init__(self, whole, cut, sems, rank, first_row=0, count=BLOCK):
         self.whole, self.cut, self.rank = whole, cut, rank
+        self.first_row, self.count = first_row, count
         self.width = whole.shape[1]
         self.sems = sems
         self.sources = [along_z(rank, 4 - step) for step in STEPS]
@@ -74,7 +76,7 @@
         self.over_x, self.over_z, self.siblings = [], [], {}
 
     def at(self, owner, low=0, high=None):
-        rows = pl.ds(pl.multiple_of(owner * BLOCK, BLOCK), BLOCK)
+        rows = pl.ds(pl.multiple_of(owner * BLOCK + self.first_row, self.count), self.count)
         if low == 0 and high is None:
             return self.whole.at[rows]
         return self.whole.at[rows, pl.ds(low, high - low)]
@@ -242,8 +244,8 @@
             sent.wait_send()
 
 
-def norm_into(inputs, gain, whole, rank):
-    @pl.loop(0, BLOCK // 16)
+def norm_into(inputs, gain, whole, rank, first_row=0, count=BLOCK):
+    @pl.loop(first_row // 16, (first_row + count) // 16)
     def _(r):
         values = inputs[pl.ds(pl.multiple_of(r * 16, 16), 16), :].astype(jnp.float32)
         mean = jnp.mean(values * values, axis=-1, keepdims=True)
@@ -252,13 +254,10 @@
 
 
 def hidden(tokens, gate_up, active, first_row, active_row):
-    @pl.loop(0, gate_up.shape[2] // TILE)
-    def _(n):
-        columns = pl.ds(pl.multiple_of(n * TILE, TILE), TILE)
-        rows_in = tokens[pl.ds(first_row, PLANE), :]
-        gate = jnp.dot(rows_in, gate_up[0, :, columns], preferred_element_type=jnp.float32)
-        up = jnp.dot(rows_in, gate_up[1, :, columns], preferred_element_type=jnp.float32)
-        active[pl.ds(active_row, PLANE), columns] = (jax.nn.silu(gate) * up).astype(jnp.bfloat16)
+    rows_in = tokens[pl.ds(first_row, PLANE), :]
+    gate = jnp.dot(rows_in, gate_up[0], preferred_element_type=jnp.float32)
+    up = jnp.dot(rows_in, gate_up[1], preferred_element_type=jnp.float32)
+    active[pl.ds(active_row, PLANE), :] = (jax.nn.silu(gate) * up).astype(jnp.bfloat16)
 
 
 def project(active, down, all_mix, partial, m, first_row, active_row, lane):
@@ -266,7 +265,7 @@
     lanes = lax.broadcasted_iota(jnp.int32, mix.shape, 1)
     weight = jnp.sum(jnp.where(lanes == lane, mix, 0.0), axis=-1, keepdims=True)
 
-    @pl.loop(0, down.shape[1] // TILE)
+    @pl.loop(0, down.shape[1] // TILE, unroll=True)
     def _(n):
         columns = pl.ds(pl.multiple_of(n * TILE, TILE), TILE)
         result = jnp.dot(
@@ -299,10 +298,8 @@
         return ref.at[pl.ds(pl.multiple_of(owner * low + k * half, half), half)]
 
     own = [gate_up.at[0], gate_up.at[1], down.at[pl.ds(0, half)], down.at[pl.ds(half, half)]]
-    parts = [functools.partial(gate_part, full_gate_up, 0), functools.partial(gate_part, full_gate_up, 1),
-             functools.partial(down_part, full_down, 0), functools.partial(down_part, full_down, 1)]
-    nearby = [functools.partial(gate_part, w_gate_up, 0), functools.partial(gate_part, w_gate_up, 1),
-              functools.partial(down_part, w_down, 0), functools.partial(down_part, w_down, 1)]
+    parts = [functools.partial(gate_part, w_gate_up, 0), functools.partial(gate_part, w_gate_up, 1),
+             functools.partial(down_part, w_down, 0), functools.partial(down_part, w_down, 1)]
 
     def sems(k, i):
         return (y_send.at[k, i], y_recv.at[k, i])
@@ -331,7 +328,8 @@
         ways[k + 1][0].start()
         ways[k][1].start()
 
-    opposite = lax.rem(place + 2, 4)
+    for k in range(4):
+        local_copy(own[k], parts[k](place), k)
     send_own(0)
     norm_into(inputs, gain, tokens, rank)
     spread = Spread(tokens, width, (d_send, d_recv), rank)
@@ -339,10 +337,6 @@
     all_mix[pl.ds(pl.multiple_of(rank * BLOCK, BLOCK), BLOCK), :] = mix[...]
     mixes = Spread(all_mix, all_mix.shape[1], (m_send, m_recv), rank)
     mixes.begin()
-    for k in range(4):
-        local_copy(own[k], parts[k](place), k)
-        local_copy(own[k], nearby[k](place), 4 + k)
-
     spreads = (spread, mixes)
     for one in spreads:
         one.forward_x_arrival()
@@ -365,16 +359,12 @@
     def land(k):
         for j in (k, k + 1):
             ways[j][1 - j % 2].wait_recv()
-            local_copy(parts[j](left), nearby[j](left), 8 + j)
-            local_copy(parts[j](right), nearby[j](right), 12 + j)
 
     def land_passed(k):
         for j in (k, k + 1):
             passes[j].wait_recv()
-            local_copy(parts[j](opposite), nearby[j](opposite), 16 + j)
 
     pass_on(0)
-    send_own(2)
     land(0)
     for i in range(3):
         for one in spreads:
@@ -384,8 +374,7 @@
         for i in range(3):
             one.wait_plane(i)
     land_passed(0)
-    pass_on(2)
-    land(2)
+    send_own(2)
     for copy in local:
         copy.wait()
     local.clear()
@@ -395,11 +384,14 @@
         row = pl.multiple_of(b * PLANE, PLANE)
         hidden(tokens, w_gate_up, active, row, row)
 
+    pass_on(2)
+    land(2)
     land_passed(2)
-    for copy in local:
-        copy.wait()
-    local.clear()
-    keep = local_copy(all_mix, mix_out, 0)
+    kept = [
+        local_copy(w_gate_up, full_gate_up, 0),
+        local_copy(w_down, full_down, 1),
+        local_copy(all_mix, mix_out, 2),
+    ]
 
     combine = Combine(partial, theirs, over_x, from_z, None, None, width, (c_send, c_recv), rank)
     order = (3, 1, 2, 0)
@@ -415,7 +407,8 @@
     combine.add_x(order[2])
     combine.add_x(order[3])
     combine.finish(inputs, out)
-    keep.wait()
+    for copy in kept:
+        copy.wait()
     for one in spreads:
         one.finish()
     for k in range(4):
@@ -460,7 +453,7 @@
             pltpu.VMEM((rows, width), jnp.bfloat16),
             pltpu.VMEM((rows, 128), jnp.float32),
             *token_scratch(width, hidden_width, rows),
-            DMA((4, 3)), DMA((4, 3)), DMA((20,)), DMA((4,)), DMA((4,)),
+            DMA((4, 3)), DMA((4, 3)), DMA((4,)), DMA((4,)), DMA((4,)),
             DMA((18,)), DMA((18,)), DMA((18,)), DMA((18,)), DMA((25,)), DMA((25,)),
         ],
         compiler_params=pltpu.CompilerParams(
@@ -482,43 +475,62 @@
         copy = pltpu.make_async_copy(src, dst, here.at[i])
         copy.start()
         loads.append(copy)
-    norm_into(inputs, gain, tokens, rank)
-    spread = Spread(tokens, cut, (d_send, d_recv), rank)
-    spread.begin()
+    spreads = []
+    for i in range(2):
+        norm_into(inputs, gain, tokens, rank, i * HALF, HALF)
+        one = Spread(tokens, cut, (d_send.at[i], d_recv.at[i]), rank, i * HALF, HALF)
+        one.begin()
+        spreads.append(one)
     combine = Combine(partial, theirs, over_x, from_z, halves, last, cut, (c_send, c_recv), rank)
 
-    def compute(m):
-        row = plane_row(rank, m)
-        hidden(tokens, w_gate_up, active, row, 0)
-        project(active, w_down, mix, partial, m, row, 0, EXPERTS + rank)
+    def up(m):
+        hidden(tokens, w_gate_up, active, plane_row(rank, m), 0)
+
+    def project_out(m):
+        project(active, w_down, mix, partial, m, plane_row(rank, m), 0, EXPERTS + rank)
         combine.to_sibling(m)
 
-    spread.forward_x_arrival()
-    for i in range(3):
-        spread.forward_z_arrival(i)
+    def far(i):
+        for one in spreads:
+            one.forward_far_arrival(i)
+
+    def wait_plane(i):
+        for one in spreads:
+            one.wait_plane(i)
+
+    for one in spreads:
+        one.forward_x_arrival()
+        for i in range(3):
+            one.forward_z_arrival(i)
     for copy in loads:
         copy.wait()
-    spread.wait_own_plane()
-    compute(0)
-    spread.forward_far_arrival(0)
-    spread.forward_far_arrival(1)
+    for one in spreads:
+        one.wait_own_plane()
+    up(0)
+    far(0)
+    project_out(0)
+    far(1)
+    wait_plane(0)
+    up(1)
+    far(2)
     combine.add_sibling(0)
-    spread.wait_plane(0)
-    compute(1)
-    spread.forward_far_arrival(2)
+    project_out(1)
+    wait_plane(1)
+    up(2)
+    combine.add_sibling(1)
+    project_out(2)
     combine.add_x(0)
-    combine.add_sibling(1)
-    spread.wait_plane(1)
-    compute(2)
+    wait_plane(2)
+    up(3)
+    combine.add_sibling(2)
+    project_out(3)
     combine.add_x(1)
-    combine.add_sibling(2)
-    spread.wait_plane(2)
-    compute(3)
+    combine.add_sibling(3)
     combine.add_x(2)
-    combine.add_sibling(3)
     combine.add_x(3)
     combine.finish(inputs, out)
-    spread.finish()
+    for one in spreads:
+        one.finish()
 
 
 def second_tick(inputs, gain, mix, full_gate_up, full_down):
@@ -534,7 +546,7 @@
             *token_scratch(width, hidden_width, PLANE),
             pltpu.VMEM((3, 2, BLOCK, width - cut), jnp.bfloat16),
             pltpu.VMEM((BLOCK, width - cut), jnp.bfloat16),
-            DMA((2,)), DMA((18,)), DMA((18,)), DMA((25,)), DMA((25,)),
+            DMA((2,)), DMA((2, 18)), DMA((2, 18)), DMA((25,)), DMA((25,)),
         ],
         compiler_params=pltpu.CompilerParams(
             collective_id=1, has_side_effects=True, vmem_limit_bytes=60 << 20

time: 355 us -> 344 us (0.969)
  Pallas kernels: 331 us -> 318 us
    pallas_call x1, Pallas kernels: 101 us -> 89.7 us  [second_tick(): pl.pallas_call(functools.partial(second_kernel, cut), out_shape=bf16(*inp...]
where the time goes in v4:
time: 344 us
  Pallas kernels  318 us (92%)
  other arithmetic  19.7 us (6%)
  waiting for transfers between devices  3.95 us (1%)
    pallas_call x1, Pallas kernels, first_tick(): pl.pallas_call(first_kernel, out_shape=(bf16(2, width, hidden_width), bf1...  228 us
    pallas_call x1, Pallas kernels, second_tick(): pl.pallas_call(functools.partial(second_kernel, cut), out_shape=bf16(*inp...  89.7 us
    select_n x3, other arithmetic, per_device(): jnp.where(moves, got.reshape(own.shape), own)  9.87 us
  transfers between devices with their start and end apart: 1, of which 1 were waited for; matrix products, arithmetic and copies ran while one was open for 3% of the time, Pallas kernels for 0%

profile of v4, /device:TPU:2, one launch (start us, length us, event | category | flops | bytes accessed | tf_op | source)
XLA Modules:
  0.0 343.7 jit_solution(10452473144230420030)
XLA Ops:
  0.6 0.7 reduce_sum.18
  1.4 0.7 bitcast_divide_fusion
  2.1 0.8 bitcast_add_fusion
  2.8 0.1 copy.17
  2.9 0.1 copy.18
  3.0 1.0 select_reduce_fusion.mix
  4.0 2.0 bitcast_select_fusion.5.inputs
  6.1 228.0 %first_tick.1 = (bf16[2,4096,768]{2,1,0:T(8,128)(2,1)}, bf16[768,4096]{1,0:T(8,128)(2,1)}, bf16[2,1024,768]{2,1,0:T(8,128)(2,1)}, bf16[192,4096]{1,0:T(8,128)(2,...) custom-call(bf16[64,4096]{1,0:T(8,128)(2,1)} %bitcast_select_fusion., ...), custom_call_target="tpu_custom_call" | custom-call | tf_op jit(solution)/shard_map/first_tick/pallas_call | solution.py:443
  234.0 1.5 collective-permute-start
  235.5 0.0 copy-done.8
  235.5 0.6 fusion
  236.1 0.0 copy-done.1
  236.1 0.0 copy-done.2
  236.1 0.0 copy-start.4
  236.1 5.0 %bitcast_select_fusion.1 = (bf16[1,1,192,4096]{3,2,1,0:T(8,128)(2,1)}, bf16[1,1,192,4096]{3,2,1,0:T(8,128)(2,1)}) fusion(bf16[1,1,192,4096]{3,2,1,0:T(8,128)(2,1)S(1)} %copy-done.2, bf16[192,4096]{1,0:T(8,128)(2,1)} %get-tuple-element.20, pred[]{:T(512)} %bitcast.11, bf16[1,1,192,4096]{3,2,1,0:T(8,128)(2,1)S(1)} %copy-done.1, ...), kind=kLoop, calls=%fused_computation.1 | loop fusion | flops 1572864 | bytes 9437185 | tf_op jit(solution)/shard_map/jit(_where)/select_n | solution.py:599
  241.2 0.0 copy-done.3
  241.2 0.0 copy-done.5
  241.2 2.1 bitcast_select_fusion.3
  243.3 0.0 copy-done.4
  243.3 2.7 bitcast_select_fusion
  246.0 4.0 %collective-permute-done = bf16[64,4096]{1,0:T(8,128)(2,1)} collective-permute-done((bf16[64,4096]{1,0:T(8,128)(2,1)}, bf16[64,4096]{1,0:T(8,128)(2,1)}, u32[]{:S(2)}, u32[]{:S(2)}) %collective-permute-start) | collective-permute-done | bytes 524320 | tf_op jit(solution)/shard_map/ppermute | solution.py:561
  250.0 1.9 bitcast_select_fusion.4.inputs
  251.9 89.7 %second_tick.1 = bf16[64,4096]{1,0:T(8,128)(2,1)} custom-call(bf16[64,4096]{1,0:T(8,128)(2,1)} %bitcast_select_fusion.4.inputs, f32[1,4096]{1,0:T(1,128)} %gain.3, f32[1024,128]{1,0:T(8,128)} %get-tuple-element.14.mix, bf16[2,4096,768]{2,1,0:T(8,128)(2,1)} %get-tuple-element.15.full_gate_up, bf16[768,4096]{1,0:T(8,128)(2,1)} %get-tuple-element.16.full_down), custom_call_target="tpu_custom_call" | custom-call | tf_op jit(solution)/shard_map/second_tick/pallas_call | solution.py:539
  341.6 2.1 maximum_bitcast_fusion
  (12 shorter events, 0.0 us)
Async XLA Ops:
  6.1 229.5 %copy-start.8 = (s32[8,1]{0,1:T(1,128)S(1)}, s32[8,1]{0,1:T(1,128)}, u32[]{:S(2)}) copy-start(s32[8,1]{0,1:T(1,128)} %param.19) | copy-start | bytes 100
  6.1 230.1 %copy-start.1 = (bf16[1,1,192,4096]{3,2,1,0:T(8,128)(2,1)S(1)}, bf16[1,1,192,4096]{3,2,1,0:T(8,128)(2,1)}, u32[]{:S(2)}) copy-start(bf16[1,1,192,4096]{3,2,1,0:T(8,128)(2,1)} %param.15) | copy-start | bytes 4718596
  6.1 230.1 %copy-start.2 = (bf16[1,1,192,4096]{3,2,1,0:T(8,128)(2,1)S(1)}, bf16[1,1,192,4096]{3,2,1,0:T(8,128)(2,1)}, u32[]{:S(2)}) copy-start(bf16[1,1,192,4096]{3,2,1,0:T(8,128)(2,1)} %param.16) | copy-start | bytes 4718596
  234.0 16.0 %collective-permute-start = (bf16[64,4096]{1,0:T(8,128)(2,1)}, bf16[64,4096]{1,0:T(8,128)(2,1)}, u32[]{:S(2)}, u32[]{:S(2)}) collective-permute-start(bf16[64,4096]{1,0:T(8,128)(2,1)} %get-tuple-element.13), channel_id=1, source_target_pairs={{0,64},{1,65},{2,66},{3,67},{4,68},{5,69},{6,70},{7,71},{8,72},{9,... | collective-permute-start | bytes 1572872 | tf_op jit(solution)/shard_map/ppermute | solution.py:561
  236.1 5.1 %copy-start.3 = (bf16[1,1,192,4096]{3,2,1,0:T(8,128)(2,1)S(1)}, bf16[1,1,192,4096]{3,2,1,0:T(8,128)(2,1)}, u32[]{:S(2)}) copy-start(bf16[1,1,192,4096]{3,2,1,0:T(8,128)(2,1)} %param.14) | copy-start | bytes 4718596
  236.1 5.1 %copy-start.5 = (bf16[192,4096]{1,0:T(8,128)(2,1)S(1)}, bf16[192,4096]{1,0:T(8,128)(2,1)}, u32[]{:S(2)}) copy-start(bf16[192,4096]{1,0:T(8,128)(2,1)} %get-tuple-element.18) | copy-start | bytes 4718596
  236.1 7.2 %copy-start.4 = (bf16[2,1024,768]{2,1,0:T(8,128)(2,1)S(1)}, bf16[2,1024,768]{2,1,0:T(8,128)(2,1)}, u32[]{:S(2)}) copy-start(bf16[2,1024,768]{2,1,0:T(8,128)(2,1)} %get-tuple-element.17) | copy-start | bytes 9437188
  241.2 2.1 copy-start
  243.3 6.7 %copy-start.6 = (bf16[2,64,4096]{2,1,0:T(8,128)(2,1)S(1)}, bf16[2,64,4096]{2,1,0:T(8,128)(2,1)}, u32[]{:S(2)}) copy-start(bf16[2,64,4096]{2,1,0:T(8,128)(2,1)} %param.10) | copy-start | bytes 3145732
  251.9 89.7 %copy-start.7 = (bf16[64,4096]{1,0:T(8,128)(2,1)S(1)}, bf16[64,4096]{1,0:T(8,128)(2,1)}, u32[]{:S(2)}) copy-start(bf16[64,4096]{1,0:T(8,128)(2,1)} %get-tuple-element.13) | copy-start | bytes 1572868

commit v5 on v4

--- a/solution.py
+++ b/solution.py
@@ -11,7 +11,8 @@
 BLOCK = 64
 PLANE = 4 * BLOCK
 HALF = BLOCK // 2
-TILE = 256
+TILE = 1024
+CHUNKS = 4
 MESH = pl.DeviceIdType.MESH
 ANY = pl.BlockSpec(memory_space=pl.ANY)
 VMEM = pl.BlockSpec(memory_space=pltpu.VMEM)
@@ -134,10 +135,10 @@
 
 
 class Combine:
-    def __init__(self, partial, theirs, over_x, from_z, halves, last, cut, sems, rank):
+    def __init__(self, partial, theirs, over_x, from_z, halves, last, columns, sems, rank):
         self.partial, self.theirs, self.over_x, self.from_z = partial, theirs, over_x, from_z
-        self.halves, self.last, self.cut, self.rank = halves, last, cut, rank
-        self.width = partial.shape[2]
+        self.halves, self.last, self.rank = halves, last, rank
+        self.low, self.cut, self.width = columns
         self.send, self.recv = sems
         self.side = lax.rem(rank // 2, 2)
         self.core = lax.rem(rank, 2)
@@ -155,9 +156,12 @@
         return pl.multiple_of((side * 2 + core) * BLOCK, BLOCK)
 
     def to_sibling(self, m):
+        columns = pl.ds(self.low, self.width - self.low)
         for dx in (1, 0):
-            src = self.partial.at[m, pl.ds(self.rows(dx, 1 - self.core), BLOCK)]
-            self.sibling[m, dx] = self.start(src, self.theirs.at[m, dx], 2 * m + dx, self.rank ^ 1)
+            src = self.partial.at[m, pl.ds(self.rows(dx, 1 - self.core), BLOCK), columns]
+            self.sibling[m, dx] = self.start(
+                src, self.theirs.at[m, dx, :, columns], 2 * m + dx, self.rank ^ 1
+            )
 
     def add_sibling(self, m):
         peer = along_z(self.rank, HOMES[m])
@@ -170,9 +174,9 @@
                 total = mine.astype(jnp.float32) + self.theirs[m, dx, rows, columns].astype(jnp.float32)
                 self.theirs[m, dx, rows, columns] = total.astype(jnp.bfloat16)
 
-            over_tiles(0, self.width, body)
+            over_tiles(self.low, self.width, body)
             if dx == 1:
-                below = pl.ds(0, self.cut)
+                below = pl.ds(self.low, self.cut - self.low)
                 self.x_copies[m] = self.start(
                     self.theirs.at[m, 1, :, below], self.over_x.at[m, :, below], 8 + m, self.rank ^ 2
                 )
@@ -190,9 +194,9 @@
             total = total + self.theirs[m, 0, rows, columns].astype(jnp.float32)
             self.over_x[m, rows, columns] = total.astype(jnp.bfloat16)
 
-        over_tiles(0, self.cut, body)
+        over_tiles(self.low, self.cut, body)
         if m:
-            below = pl.ds(0, self.cut)
+            below = pl.ds(self.low, self.cut - self.low)
             self.z_copies[m] = self.start(
                 self.over_x.at[m, :, below], self.from_z.at[m - 1, :, below], 20 + m,
                 along_z(self.rank, HOMES[m]),
@@ -229,7 +233,7 @@
                 total = total + self.from_z[m, rows, columns].astype(jnp.float32)
             out[rows, columns] = total.astype(jnp.bfloat16)
 
-        over_tiles(0, cut, near)
+        over_tiles(self.low, cut, near)
         if cut < width:
             copy.wait_recv()
 
@@ -240,6 +244,8 @@
                 out[rows, columns] = total.astype(jnp.bfloat16)
 
             over_tiles(cut, width, far)
+
+    def drain(self):
         for sent in self.sent:
             sent.wait_send()
 
@@ -260,14 +266,13 @@
     active[pl.ds(active_row, PLANE), :] = (jax.nn.silu(gate) * up).astype(jnp.bfloat16)
 
 
-def project(active, down, all_mix, partial, m, first_row, active_row, lane):
+def project(active, down, all_mix, partial, m, first_row, active_row, lane, low, high):
     mix = all_mix[pl.ds(first_row, PLANE), :]
     lanes = lax.broadcasted_iota(jnp.int32, mix.shape, 1)
     weight = jnp.sum(jnp.where(lanes == lane, mix, 0.0), axis=-1, keepdims=True)
 
-    @pl.loop(0, down.shape[1] // TILE, unroll=True)
-    def _(n):
-        columns = pl.ds(pl.multiple_of(n * TILE, TILE), TILE)
+    for start in range(low, high, TILE):
+        columns = pl.ds(start, TILE)
         result = jnp.dot(
             active[pl.ds(active_row, PLANE), :], down[:, columns], preferred_element_type=jnp.float32
         )
@@ -276,6 +281,15 @@
 
 def plane_row(rank, m):
     return pl.multiple_of(along_z(rank, HOMES[m]) // 4 * PLANE, PLANE)
+
+
+def early(ref):
+    return ref.at[pl.ds(0, ref.shape[0] // 3)]
+
+
+def late(ref):
+    middle = ref.shape[0] // 3
+    return ref.at[pl.ds(middle, ref.shape[0] - middle)]
 
 
 def first_kernel(
@@ -294,12 +308,16 @@
     def gate_part(ref, k, owner):
         return ref.at[k, pl.ds(pl.multiple_of(owner * deep, deep), deep)]
 
+    chunk = width // CHUNKS
+
     def down_part(ref, k, owner):
-        return ref.at[pl.ds(pl.multiple_of(owner * low + k * half, half), half)]
-
-    own = [gate_up.at[0], gate_up.at[1], down.at[pl.ds(0, half)], down.at[pl.ds(half, half)]]
-    parts = [functools.partial(gate_part, w_gate_up, 0), functools.partial(gate_part, w_gate_up, 1),
-             functools.partial(down_part, w_down, 0), functools.partial(down_part, w_down, 1)]
+        row, column = owner * low + k % 2 * half, k // 2 * chunk
+        return ref.at[pl.ds(pl.multiple_of(row, half), half), pl.ds(column, chunk)]
+
+    count = 2 + 2 * CHUNKS
+    own = [gate_up.at[0], gate_up.at[1]] + [down_part(down, k, 0) for k in range(2 * CHUNKS)]
+    parts = [functools.partial(gate_part, w_gate_up, 0), functools.partial(gate_part, w_gate_up, 1)]
+    parts += [functools.partial(down_part, w_down, k) for k in range(2 * CHUNKS)]
 
     def sems(k, i):
         return (y_send.at[k, i], y_recv.at[k, i])
@@ -307,12 +325,12 @@
     ways = [
         (remote(own[k], parts[k](place), sems(k, 0), {"dp": right}),
          remote(own[k], parts[k](place), sems(k, 1), {"dp": left}))
-        for k in range(4)
+        for k in range(count)
     ]
     passes = [
         remote(parts[k](left), parts[k](left), sems(k, 2), {"dp": right}) if k % 2 == 0
         else remote(parts[k](right), parts[k](right), sems(k, 2), {"dp": left})
-        for k in range(4)
+        for k in range(count)
     ]
     local = []
 
@@ -328,7 +346,7 @@
         ways[k + 1][0].start()
         ways[k][1].start()
 
-    for k in range(4):
+    for k in range(count):
         local_copy(own[k], parts[k](place), k)
     send_own(0)
     norm_into(inputs, gain, tokens, rank)
@@ -345,7 +363,7 @@
             one.forward_z_arrival(i)
     trades = []
     for i, (src, dst) in enumerate(
-        ((gate_up, got_gate_up), (down, got_down), (first, got_first), (second, got_second))
+        ((gate_up, got_gate_up), (down, got_down), (first, got_first), (early(second), early(got_second)))
     ):
         copy = remote(src, dst, (trade_send.at[i], trade_recv.at[i]), {"expert": rank ^ 8})
         copy.start()
@@ -375,43 +393,62 @@
             one.wait_plane(i)
     land_passed(0)
     send_own(2)
+    send_own(4)
     for copy in local:
         copy.wait()
     local.clear()
+
+    kept = []
+
+    def keep(src, dst, i):
+        kept.append(pltpu.make_async_copy(src, dst, here.at[i]))
+        kept[-1].start()
 
     @pl.loop(0, 4)
     def _(b):
         row = pl.multiple_of(b * PLANE, PLANE)
         hidden(tokens, w_gate_up, active, row, row)
 
-    pass_on(2)
-    land(2)
-    land_passed(2)
-    kept = [
-        local_copy(w_gate_up, full_gate_up, 0),
-        local_copy(w_down, full_down, 1),
-        local_copy(all_mix, mix_out, 2),
+    combines = [
+        Combine(
+            partial, theirs, over_x, from_z, None, None, (c * chunk, (c + 1) * chunk, (c + 1) * chunk),
+            (c_send.at[c], c_recv.at[c]), rank,
+        )
+        for c in range(CHUNKS)
     ]
-
-    combine = Combine(partial, theirs, over_x, from_z, None, None, width, (c_send, c_recv), rank)
     order = (3, 1, 2, 0)
-    for i, m in enumerate(order):
-        row = plane_row(rank, m)
-        project(active, w_down, all_mix, partial, m, row, row, rank)
-        combine.to_sibling(m)
-        if i:
-            combine.add_sibling(order[i - 1])
-        if i > 1:
-            combine.add_x(order[i - 2])
-    combine.add_sibling(order[3])
-    combine.add_x(order[2])
-    combine.add_x(order[3])
-    combine.finish(inputs, out)
+    for c in range(CHUNKS):
+        pass_on(2 + 2 * c)
+        if c + 2 < CHUNKS:
+            send_own(6 + 2 * c)
+        land(2 + 2 * c)
+        land_passed(2 + 2 * c)
+        for m in order:
+            row = plane_row(rank, m)
+            project(
+                active, w_down, all_mix, partial, m, row, row, rank, c * chunk, (c + 1) * chunk
+            )
+            combines[c].to_sibling(m)
+        for m in order:
+            combines[c].add_sibling(m)
+        if c:
+            for m in order:
+                combines[c - 1].add_x(m)
+        if c == 1:
+            keep(w_gate_up, full_gate_up, 0)
+            keep(all_mix, mix_out, 1)
+    keep(w_down, full_down, 2)
+    for m in order:
+        combines[CHUNKS - 1].add_x(m)
+    for one in combines:
+        one.finish(inputs, out)
+    for one in combines:
+        one.drain()
     for copy in kept:
         copy.wait()
     for one in spreads:
         one.finish()
-    for k in range(4):
+    for k in range(count):
         ways[k][0].wait_send()
         ways[k][1].wait_send()
         passes[k].wait_send()
@@ -453,8 +490,8 @@
             pltpu.VMEM((rows, width), jnp.bfloat16),
             pltpu.VMEM((rows, 128), jnp.float32),
             *token_scratch(width, hidden_width, rows),
-            DMA((4, 3)), DMA((4, 3)), DMA((4,)), DMA((4,)), DMA((4,)),
-            DMA((18,)), DMA((18,)), DMA((18,)), DMA((18,)), DMA((25,)), DMA((25,)),
+            DMA((2 + 2 * CHUNKS, 3)), DMA((2 + 2 * CHUNKS, 3)), DMA((2 + 2 * CHUNKS,)), DMA((4,)), DMA((4,)),
+            DMA((18,)), DMA((18,)), DMA((18,)), DMA((18,)), DMA((CHUNKS, 25)), DMA((CHUNKS, 25)),
         ],
         compiler_params=pltpu.CompilerParams(
             collective_id=0, has_side_effects=True, vmem_limit_bytes=60 << 20
@@ -464,9 +501,9 @@
 
 
 def second_kernel(
-    cut, inputs, gain, mix, full_gate_up, full_down, out,
+    cut, inputs, gain, mix, full_gate_up, full_down, second, _, out, got_second,
     tokens, w_gate_up, w_down, active, partial, theirs, over_x, from_z, halves, last,
-    here, d_send, d_recv, c_send, c_recv,
+    here, trade_send, trade_recv, d_send, d_recv, c_send, c_recv,
 ):
     rank = lax.axis_index("expert")
     greet(group(rank))
@@ -481,13 +518,14 @@
         one = Spread(tokens, cut, (d_send.at[i], d_recv.at[i]), rank, i * HALF, HALF)
         one.begin()
         spreads.append(one)
-    combine = Combine(partial, theirs, over_x, from_z, halves, last, cut, (c_send, c_recv), rank)
+    columns = (0, cut, inputs.shape[1])
+    combine = Combine(partial, theirs, over_x, from_z, halves, last, columns, (c_send, c_recv), rank)
 
     def up(m):
         hidden(tokens, w_gate_up, active, plane_row(rank, m), 0)
 
     def project_out(m):
-        project(active, w_down, mix, partial, m, plane_row(rank, m), 0, EXPERTS + rank)
+        project(active, w_down, mix, partial, m, plane_row(rank, m), 0, EXPERTS + rank, 0, inputs.shape[1])
         combine.to_sibling(m)
 
     def far(i):
@@ -502,6 +540,10 @@
         one.forward_x_arrival()
         for i in range(3):
             one.forward_z_arrival(i)
+    trade = remote(
+        late(second), late(got_second), (trade_send.at[0], trade_recv.at[0]), {"expert": rank ^ 8}
+    )
+    trade.start()
     for copy in loads:
         copy.wait()
     for one in spreads:
@@ -529,30 +571,34 @@
     combine.add_x(2)
     combine.add_x(3)
     combine.finish(inputs, out)
+    combine.drain()
     for one in spreads:
         one.finish()
-
-
-def second_tick(inputs, gain, mix, full_gate_up, full_down):
+    trade.wait_recv()
+    trade.wait_send()
+
+
+def second_tick(inputs, gain, mix, full_gate_up, full_down, second, got_second):
     width, hidden_width = inputs.shape[1], full_gate_up.shape[2]
     cut = 2560
     return pl.pallas_call(
         functools.partial(second_kernel, cut),
-        out_shape=bf16(*inputs.shape),
-        in_specs=[VMEM] * 3 + [ANY] * 2,
-        out_specs=VMEM,
+        out_shape=(bf16(*inputs.shape), bf16(*second.shape)),
+        in_specs=[VMEM] * 3 + [ANY] * 4,
+        out_specs=[VMEM, ANY],
+        input_output_aliases={6: 1},
         scratch_shapes=[
             pltpu.VMEM((EXPERTS * BLOCK, width), jnp.bfloat16),
             *token_scratch(width, hidden_width, PLANE),
             pltpu.VMEM((3, 2, BLOCK, width - cut), jnp.bfloat16),
             pltpu.VMEM((BLOCK, width - cut), jnp.bfloat16),
-            DMA((2,)), DMA((2, 18)), DMA((2, 18)), DMA((25,)), DMA((25,)),
+            DMA((2,)), DMA((1,)), DMA((1,)), DMA((2, 18)), DMA((2, 18)), DMA((25,)), DMA((25,)),
         ],
         compiler_params=pltpu.CompilerParams(
             collective_id=1, has_side_effects=True, vmem_limit_bytes=60 << 20
         ),
         name="second_tick",
-    )(inputs, gain, mix, full_gate_up, full_down)
+    )(inputs, gain, mix, full_gate_up, full_down, second, got_second)
 
 
 def shifted(value, axis, distance):
@@ -590,7 +636,9 @@
     )
     arrived = shifted(tick_zero, "section", 1)
     second_input = jnp.where(section_index == 0, fresh_tokens[1], arrived)
-    tick_one = second_tick(second_input, norm_weight, all_mix, full_gate_up, full_down)
+    tick_one, traded[3] = second_tick(
+        second_input, norm_weight, all_mix, full_gate_up, full_down, second_moment[0, 0], traded[3]
+    )
     layer_out = jnp.stack([tick_zero, tick_one])[None]
 
     moves = trade_flags[own_rank % half_span, 0] == 1

time: 344 us -> 329 us (0.956)
  Pallas kernels: 318 us -> 300 us
    pallas_call x1, Pallas kernels: 228 us -> 207 us  [first_tick(): pl.pallas_call(first_kernel, out_shape=(bf16(2, width, hidden_width), bf1...]
    pallas_call x1, Pallas kernels: 89.7 us -> 93.3 us  [second_tick(): pl.pallas_call(functools.partial(second_kernel, cut), out_shape=(bf16(*in...]
where the time goes in v5:
time: 329 us
  Pallas kernels  300 us (91%)
  other arithmetic  20.2 us (6%)
  waiting for transfers between devices  5.9 us (2%)
    pallas_call x1, Pallas kernels, first_tick(): pl.pallas_call(first_kernel, out_shape=(bf16(2, width, hidden_width), bf1...  207 us
    pallas_call x1, Pallas kernels, second_tick(): pl.pallas_call(functools.partial(second_kernel, cut), out_shape=(bf16(*in...  93.3 us
    select_n x3, other arithmetic, per_device(): jnp.where(moves, got.reshape(own.shape), own)  11.4 us
  transfers between devices with their start and end apart: 1, of which 1 were waited for; matrix products, arithmetic and copies ran while one was open for 3% of the time, Pallas kernels for 0%

profile of v5, /device:TPU:2, one launch (start us, length us, event | category | flops | bytes accessed | tf_op | source)
XLA Modules:
  0.0 328.7 jit_solution(13853965939237593971)
XLA Ops:
  0.6 0.7 reduce_sum.18
  1.4 0.7 bitcast_divide_fusion
  2.1 0.8 bitcast_add_fusion
  2.8 0.1 copy.18
  2.9 0.1 copy.19
  3.0 1.0 select_reduce_fusion.mix
  4.0 2.0 bitcast_select_fusion.5.inputs
  6.1 206.9 %first_tick.1 = (bf16[2,4096,768]{2,1,0:T(8,128)(2,1)}, bf16[768,4096]{1,0:T(8,128)(2,1)}, bf16[2,1024,768]{2,1,0:T(8,128)(2,1)}, bf16[192,4096]{1,0:T(8,128)(2,...) custom-call(bf16[64,4096]{1,0:T(8,128)(2,1)} %bitcast_select_fusion., ...), custom_call_target="tpu_custom_call" | custom-call | tf_op jit(solution)/shard_map/first_tick/pallas_call | solution.py:480
  212.9 1.5 collective-permute-start
  214.4 0.0 copy-done.8
  214.4 0.7 fusion
  215.1 0.0 copy-done.2
  215.1 0.0 copy-done.3
  215.1 5.1 %bitcast_select_fusion.2 = (bf16[1,1,192,4096]{3,2,1,0:T(8,128)(2,1)}, bf16[1,1,192,4096]{3,2,1,0:T(8,128)(2,1)}) fusion(bf16[1,1,192,4096]{3,2,1,0:T(8,128)(2,1)S(1)} %copy-done.3, bf16[192,4096]{1,0:T(8,128)(2,1)} %get-tuple-element.23, pred[]{:T(512)} %bitcast.11, bf16[1,1,192,4096]{3,2,1,0:T(8,128)(2,1)S(1)} %copy-done.2, ...), kind=kLoop, calls=%fused_computation.2 | loop fusion | flops 1572864 | bytes 9437185 | tf_op jit(solution)/shard_map/jit(_where)/select_n | solution.py:647
  220.2 0.0 copy-done.1
  220.2 0.0 copy-done.4
  220.2 2.8 bitcast_select_fusion
  223.0 5.9 %collective-permute-done = bf16[64,4096]{1,0:T(8,128)(2,1)} collective-permute-done((bf16[64,4096]{1,0:T(8,128)(2,1)}, bf16[64,4096]{1,0:T(8,128)(2,1)}, u32[]{:S(2)}, u32[]{:S(2)}) %collective-permute-start) | collective-permute-done | bytes 524320 | tf_op jit(solution)/shard_map/ppermute | solution.py:607
  228.9 0.0 copy-done.5
  228.9 1.9 bitcast_select_fusion.4.inputs
  230.8 93.3 %second_tick.1 = (bf16[64,4096]{1,0:T(8,128)(2,1)}, bf16[192,4096]{1,0:T(8,128)(2,1)}) custom-call(bf16[64,4096]{1,0:T(8,128)(2,1)} %bitcast_select_fusion.4.inputs, f32[1,4096]{1,0:T(1,128)} %gain.3, f32[1024,128]{1,0:T(8,128)} %get-tuple-element.16.mix, bf16[2,4096,768]{2,1,0:T(8,128)(2,1)} %get-tuple-element.17.full_gate_up, ...), custom_call_target="tpu_custom_call", output_to_operand_aliasing={{1}: (6, {})} | custom-call | tf_op jit(solution)/shard_map/second_tick/pallas_call | solution.py:584
  324.1 0.0 copy-done
  324.1 3.5 %bitcast_select_fusion.1 = bf16[1,1,192,4096]{3,2,1,0:T(8,128)(2,1)} fusion(bf16[1,1,192,4096]{3,2,1,0:T(8,128)(2,1)S(1)} %copy-done, bf16[192,4096]{1,0:T(8,128)(2,1)} %get-tuple-element.24, pred[]{:T(512)} %bitcast.11), kind=kLoop, calls=%fused_computation.1 | loop fusion | flops 786432 | bytes 4718593 | tf_op jit(solution)/shard_map/jit(_where)/select_n | solution.py:647
  327.6 1.1 maximum_bitcast_fusion
  (12 shorter events, 0.0 us)
Async XLA Ops:
  6.1 208.4 %copy-start.8 = (s32[8,1]{0,1:T(1,128)S(1)}, s32[8,1]{0,1:T(1,128)}, u32[]{:S(2)}) copy-start(s32[8,1]{0,1:T(1,128)} %param.19) | copy-start | bytes 100
  6.1 209.0 %copy-start.2 = (bf16[1,1,192,4096]{3,2,1,0:T(8,128)(2,1)S(1)}, bf16[1,1,192,4096]{3,2,1,0:T(8,128)(2,1)}, u32[]{:S(2)}) copy-start(bf16[1,1,192,4096]{3,2,1,0:T(8,128)(2,1)} %param.14) | copy-start | bytes 4718596
  6.1 209.0 %copy-start.3 = (bf16[1,1,192,4096]{3,2,1,0:T(8,128)(2,1)S(1)}, bf16[1,1,192,4096]{3,2,1,0:T(8,128)(2,1)}, u32[]{:S(2)}) copy-start(bf16[1,1,192,4096]{3,2,1,0:T(8,128)(2,1)} %param.15) | copy-start | bytes 4718596
  212.9 16.0 %collective-permute-start = (bf16[64,4096]{1,0:T(8,128)(2,1)}, bf16[64,4096]{1,0:T(8,128)(2,1)}, u32[]{:S(2)}, u32[]{:S(2)}) collective-permute-start(bf16[64,4096]{1,0:T(8,128)(2,1)} %get-tuple-element.15), channel_id=1, source_target_pairs={{0,64},{1,65},{2,66},{3,67},{4,68},{5,69},{6,70},{7,71},{8,72},{9,... | collective-permute-start | bytes 1572872 | tf_op jit(solution)/shard_map/ppermute | solution.py:607
  215.1 5.1 %copy-start.1 = (bf16[1,1,2,1024,768]{4,3,2,1,0:T(8,128)(2,1)S(1)}, bf16[1,1,2,1024,768]{4,3,2,1,0:T(8,128)(2,1)}, u32[]{:S(2)}) copy-start(bf16[1,1,2,1024,768]{4,3,2,1,0:T(8,128)(2,1)} %param.13) | copy-start | bytes 9437188
  215.1 5.1 %copy-start.4 = (bf16[2,1024,768]{2,1,0:T(8,128)(2,1)S(1)}, bf16[2,1024,768]{2,1,0:T(8,128)(2,1)}, u32[]{:S(2)}) copy-start(bf16[2,1024,768]{2,1,0:T(8,128)(2,1)} %get-tuple-element.21) | copy-start | bytes 9437188
  220.2 8.7 %copy-start.5 = (bf16[2,64,4096]{2,1,0:T(8,128)(2,1)S(1)}, bf16[2,64,4096]{2,1,0:T(8,128)(2,1)}, u32[]{:S(2)}) copy-start(bf16[2,64,4096]{2,1,0:T(8,128)(2,1)} %param.10) | copy-start | bytes 3145732
  230.8 93.3 %copy-start = (bf16[1,1,192,4096]{3,2,1,0:T(8,128)(2,1)S(1)}, bf16[1,1,192,4096]{3,2,1,0:T(8,128)(2,1)}, u32[]{:S(2)}) copy-start(bf16[1,1,192,4096]{3,2,1,0:T(8,128)(2,1)} %param.16) | copy-start | bytes 4718596
  324.1 3.5 %copy-start.6 = (bf16[64,4096]{1,0:T(8,128)(2,1)S(1)}, bf16[64,4096]{1,0:T(8,128)(2,1)}, u32[]{:S(2)}) copy-start(bf16[64,4096]{1,0:T(8,128)(2,1)} %get-tuple-element.15) | copy-start | bytes 1572868
  324.1 3.5 %copy-start.7 = (bf16[64,4096]{1,0:T(8,128)(2,1)S(1)}, bf16[64,4096]{1,0:T(8,128)(2,1)}, u32[]{:S(2)}) copy-start(bf16[64,4096]{1,0:T(8,128)(2,1)} %get-tuple-element.20) | copy-start | bytes 1572868
